TPU v7x, 512 devices: a whole 4x8x8 slice. The times are simulated.
512 devices in a mesh: slab: 128 (over y, z, core), col: 4 (over x).
Axes of the slice: x: 4, y: 8, z: 8, core: 2. Of those that a mesh axis runs over, the one named last changes fastest.
Arguments:
- wave_amplitudes: float32 [128, 512, 128], P('slab', 'col'), may hold values from -6 to 6
- energy_block_per_segment: float32 [128, 512, 512], P('slab', 'col'), as said below
- tunnel_coupling_block: float32 [128, 512, 512], P('slab', 'col'), may hold values from -0.25 to 0.25
- reduced_block_reciprocal: float32 [128, 2, 512, 512], P('slab', None, 'col'), may hold values from -0.1875 to 0.1875
- beneath_reduce_multiplier: float32 [128, 2, 512, 512], P('slab', None, 'col'), may hold values from -0.09375 to 0.09375
- above_reduce_multiplier: float32 [128, 2, 512, 512], P('slab', None, 'col'), may hold values from -0.09375 to 0.09375
- beneath_solve_multiplier: float32 [128, 2, 512, 512], P('slab', None, 'col'), may hold values from -0.09375 to 0.09375
- above_solve_multiplier: float32 [128, 2, 512, 512], P('slab', None, 'col'), may hold values from -0.09375 to 0.09375
Outputs:
- psi_next: float32 [128, 512, 128], P('slab', 'col')
Inputs may be any that keep to these rules, and one draw needn't show every extreme that they name: energy_block_per_segment[s] is a symmetric matrix for every slab s.
All inputs are finite; a program needn't handle non-finite values.
Results may differ from a plain program's by a relative error of at most 0.00011.
Values sent between devices are 32-bit elements; how exact they have to be, the bound alone decides.
A program may use at most 64 MiB of HBM per device.

v0:
```python
import jax
import jax.numpy as jnp
from jax import lax
from jax.sharding import PartitionSpec as P

half_step = 0.5
highest = lax.Precision.HIGHEST


def from_behind(block, axis, distance):
    devices = range(lax.axis_size(axis))
    route = [(i - distance, i) for i in devices if i - distance in devices]
    return lax.ppermute(block, axis, route)


def rotate(values):
    column = lax.broadcasted_iota(jnp.int32, values.shape, values.ndim - 1)
    return jnp.where(column % 2 == 0, -jnp.roll(values, -1, axis=-1), jnp.roll(values, 1, axis=-1))


def plain_dot(left, right):
    return jnp.dot(left, right, precision=highest, preferred_element_type=jnp.float32)


def transposed_dot(left, right):
    return lax.dot_general(
        left, right, (((0,), (0,)), ((), ())), precision=highest, preferred_element_type=jnp.float32
    )


def complex_matmul(block, vectors):
    return plain_dot(block[0], vectors) + rotate(plain_dot(block[1], vectors))


def slab_step(values, tier_spacing):
    return from_behind(values, "slab", tier_spacing)


def gather_rows(values):
    return lax.all_gather(values, "col", axis=0, tiled=True)


def per_device(
    wave_amplitudes,
    energy_block_per_segment,
    tunnel_coupling_block,
    reduced_block_reciprocal,
    beneath_reduce_multiplier,
    above_reduce_multiplier,
    beneath_solve_multiplier,
    above_solve_multiplier,
):
    states = wave_amplitudes[0]
    slab_index = lax.axis_index("slab")
    level_total = lax.axis_size("slab").bit_length() - 1
    up_rows = tunnel_coupling_block[0]
    next_shard = slab_step(states, -1)
    prev_shard = slab_step(states, 1)
    psi_full, next_full, prev_full = (
        lax.all_gather(states, "col", axis=0, tiled=True),
        lax.all_gather(next_shard, "col", axis=0, tiled=True),
        lax.all_gather(prev_shard, "col", axis=0, tiled=True),
    )
    below_rows = from_behind(up_rows, "slab", 1)
    below_cols = lax.all_to_all(below_rows, "col", split_axis=1, concat_axis=0, tiled=True)
    prev_term = transposed_dot(below_cols, prev_full)
    ham_psi = (
        plain_dot(energy_block_per_segment[0], psi_full) + plain_dot(up_rows, next_full) + prev_term
    )
    reduced = states - half_step * rotate(ham_psi)
    pivot_block = reduced_block_reciprocal[0]
    beneath_removal = beneath_reduce_multiplier[0]
    above_removal = above_reduce_multiplier[0]
    lower_back = beneath_solve_multiplier[0]
    upper_back = above_solve_multiplier[0]
    zeros_vec = jnp.zeros_like(states)
    pivot_part = zeros_vec
    for level_id in range(level_total):
        tier_spacing = 2**level_id
        active = slab_index % (2 * tier_spacing) == tier_spacing
        reduced_full = gather_rows(reduced)

        def eliminate(present_tier):
            return (
                complex_matmul(pivot_block, present_tier),
                complex_matmul(beneath_removal, present_tier),
                complex_matmul(above_removal, present_tier),
            )

        def pass_case(present_tier):
            return (zeros_vec, zeros_vec, zeros_vec)

        pivot_piece, heading_beneath, heading_above = lax.cond(
            active, eliminate, pass_case, reduced_full
        )
        pivot_part = jnp.where(active, pivot_piece, pivot_part)
        reduced = (
            reduced
            - slab_step(heading_beneath, -tier_spacing)
            - slab_step(heading_above, tier_spacing)
        )
    is_root = slab_index == 0
    root_full = gather_rows(reduced)

    def root_solve(present_tier):
        return complex_matmul(pivot_block, present_tier)

    def root_pass(present_tier):
        return zeros_vec

    pivot_part = jnp.where(is_root, lax.cond(is_root, root_solve, root_pass, root_full), pivot_part)
    solved = jnp.where(is_root, pivot_part, zeros_vec)
    for level_id in reversed(range(level_total)):
        tier_spacing = 2**level_id
        active = slab_index % (2 * tier_spacing) == tier_spacing
        lower_in = slab_step(solved, tier_spacing)
        upper_in = slab_step(solved, -tier_spacing)
        lower_full, upper_full = (
            lax.all_gather(lower_in, "col", axis=0, tiled=True),
            lax.all_gather(upper_in, "col", axis=0, tiled=True),
        )

        def settle(pair_in):
            return (
                pivot_part
                - complex_matmul(lower_back, pair_in[0])
                - complex_matmul(upper_back, pair_in[1])
            )

        def keep_case(pair_in):
            return solved

        solved = lax.cond(active, settle, keep_case, (lower_full, upper_full))
    return solved[None]


def solution(mesh):
    placed = (
        P("slab", "col", None),
        P("slab", "col", None),
        P("slab", "col", None),
        P("slab", None, "col", None),
        P("slab", None, "col", None),
        P("slab", None, "col", None),
        P("slab", None, "col", None),
        P("slab", None, "col", None),
    )
    return jax.shard_map(
        per_device, mesh=mesh, in_specs=placed, out_specs=P("slab", "col", None), check_vma=False
    )
```

profile of v0, /device:TPU:32, one launch (start us, length us, event | category | flops | bytes accessed | tf_op | source)
XLA Modules:
  0.0 499.4 jit_solution(15847063900664195438)
XLA Ops:
  16.3 12.6 %all-gather = f32[1,512,128]{2,1,0:T(8,128)S(1)} all-gather(f32[1,128,128]{2,1,0:T(8,128)S(1)} %copy-done.7), channel_id=2, replica_groups=mesh['slab'=128,'col'=4] {'col'}, dimensions={1}, use_global_device_ids=true | all-gather | bytes 327680 | tf_op jit(solution)/shard_map/all_gather | solution.py:60
  29.5 12.5 %all_gather.76 = f32[512,128]{0,1:T(8,128)S(1)} all-gather(f32[128,128]{0,1:T(8,128)S(1)} %collective-permute-done), channel_id=1, replica_groups=mesh['slab'=128,'col'=4] {'col'}, dimensions={0}, use_global_device_ids=true | all-gather | bytes 327680 | tf_op jit(solution)/shard_map/all_gather | solution.py:61
  42.0 12.2 %all_gather.77 = f32[512,128]{0,1:T(8,128)S(1)} all-gather(f32[128,128]{0,1:T(8,128)S(1)} %collective-permute-done.2), channel_id=1, replica_groups=mesh['slab'=128,'col'=4] {'col'}, dimensions={0}, use_global_device_ids=true | all-gather | bytes 327680 | tf_op jit(solution)/shard_map/all_gather | solution.py:62
  65.5 12.3 %all_gather.78 = f32[512,128]{0,1:T(8,128)S(1)} all-gather(f32[128,128]{0,1:T(8,128)S(1)} %fusion.237), channel_id=1, replica_groups=mesh['slab'=128,'col'=4] {'col'}, dimensions={0}, use_global_device_ids=true | all-gather | bytes 327680 | tf_op jit(solution)/shard_map/all_gather | solution.py:40
  90.0 12.3 %all_gather.79 = f32[512,128]{0,1:T(8,128)S(1)} all-gather(f32[128,128]{0,1:T(8,128)S(1)} %subtract_subtract_fusion.6), channel_id=1, replica_groups=mesh['slab'=128,'col'=4] {'col'}, dimensions={0}, use_global_device_ids=true | all-gather | bytes 327680 | tf_op jit(solution)/shard_map/all_gather | solution.py:40
  118.3 12.3 %all_gather.80 = f32[512,128]{0,1:T(8,128)S(1)} all-gather(f32[128,128]{0,1:T(8,128)S(1)} %subtract_subtract_fusion.5), channel_id=1, replica_groups=mesh['slab'=128,'col'=4] {'col'}, dimensions={0}, use_global_device_ids=true | all-gather | bytes 327680 | tf_op jit(solution)/shard_map/all_gather | solution.py:40
  143.5 12.3 %all_gather.81 = f32[512,128]{0,1:T(8,128)S(1)} all-gather(f32[128,128]{0,1:T(8,128)S(1)} %subtract_subtract_fusion.4), channel_id=1, replica_groups=mesh['slab'=128,'col'=4] {'col'}, dimensions={0}, use_global_device_ids=true | all-gather | bytes 327680 | tf_op jit(solution)/shard_map/all_gather | solution.py:40
  170.9 12.4 %all_gather.82 = f32[512,128]{0,1:T(8,128)S(1)} all-gather(f32[128,128]{0,1:T(8,128)S(1)} %subtract_subtract_fusion.3), channel_id=1, replica_groups=mesh['slab'=128,'col'=4] {'col'}, dimensions={0}, use_global_device_ids=true | all-gather | bytes 327680 | tf_op jit(solution)/shard_map/all_gather | solution.py:40
  195.5 12.5 %all_gather.83 = f32[512,128]{0,1:T(8,128)S(1)} all-gather(f32[128,128]{0,1:T(8,128)S(1)} %subtract_subtract_fusion.2), channel_id=1, replica_groups=mesh['slab'=128,'col'=4] {'col'}, dimensions={0}, use_global_device_ids=true | all-gather | bytes 327680 | tf_op jit(solution)/shard_map/all_gather | solution.py:40
  218.9 12.3 %all_gather.84 = f32[512,128]{0,1:T(8,128)S(1)} all-gather(f32[128,128]{0,1:T(8,128)S(1)} %subtract_subtract_fusion.1), channel_id=1, replica_groups=mesh['slab'=128,'col'=4] {'col'}, dimensions={0}, use_global_device_ids=true | all-gather | bytes 327680 | tf_op jit(solution)/shard_map/all_gather | solution.py:40
  245.6 12.3 %all_gather.85 = f32[512,128]{0,1:T(8,128)S(1)} all-gather(f32[128,128]{0,1:T(8,128)S(1)} %subtract_subtract_fusion), channel_id=1, replica_groups=mesh['slab'=128,'col'=4] {'col'}, dimensions={0}, use_global_device_ids=true | all-gather | bytes 327680 | tf_op jit(solution)/shard_map/all_gather | solution.py:40
  268.1 12.2 %all_gather.86 = f32[512,128]{1,0:T(8,128)S(1)} all-gather(f32[128,128]{1,0:T(8,128)S(1)} %collective-permute-done.17), channel_id=1, replica_groups=mesh['slab'=128,'col'=4] {'col'}, dimensions={0}, use_global_device_ids=true | all-gather | bytes 327680 | tf_op jit(solution)/shard_map/all_gather | solution.py:119
  280.4 12.2 %all_gather.87 = f32[512,128]{1,0:T(8,128)S(1)} all-gather(f32[128,128]{1,0:T(8,128)S(1)} %collective-permute-done.18), channel_id=1, replica_groups=mesh['slab'=128,'col'=4] {'col'}, dimensions={0}, use_global_device_ids=true | all-gather | bytes 327680 | tf_op jit(solution)/shard_map/all_gather | solution.py:120
  303.0 12.2 %all_gather.88 = f32[512,128]{1,0:T(8,128)S(1)} all-gather(f32[128,128]{1,0:T(8,128)S(1)} %collective-permute-done.19), channel_id=1, replica_groups=mesh['slab'=128,'col'=4] {'col'}, dimensions={0}, use_global_device_ids=true | all-gather | bytes 327680 | tf_op jit(solution)/shard_map/all_gather | solution.py:119
  315.3 12.2 %all_gather.89 = f32[512,128]{1,0:T(8,128)S(1)} all-gather(f32[128,128]{1,0:T(8,128)S(1)} %collective-permute-done.20), channel_id=1, replica_groups=mesh['slab'=128,'col'=4] {'col'}, dimensions={0}, use_global_device_ids=true | all-gather | bytes 327680 | tf_op jit(solution)/shard_map/all_gather | solution.py:120
  334.9 12.2 %all_gather.90 = f32[512,128]{1,0:T(8,128)S(1)} all-gather(f32[128,128]{1,0:T(8,128)S(1)} %collective-permute-done.21), channel_id=1, replica_groups=mesh['slab'=128,'col'=4] {'col'}, dimensions={0}, use_global_device_ids=true | all-gather | bytes 327680 | tf_op jit(solution)/shard_map/all_gather | solution.py:119
  347.1 12.6 %all_gather.91 = f32[512,128]{1,0:T(8,128)S(1)} all-gather(f32[128,128]{1,0:T(8,128)S(1)} %collective-permute-done.22), channel_id=1, replica_groups=mesh['slab'=128,'col'=4] {'col'}, dimensions={0}, use_global_device_ids=true | all-gather | bytes 327680 | tf_op jit(solution)/shard_map/all_gather | solution.py:120
  371.9 12.4 %all_gather.92 = f32[512,128]{1,0:T(8,128)S(1)} all-gather(f32[128,128]{1,0:T(8,128)S(1)} %collective-permute-done.23), channel_id=1, replica_groups=mesh['slab'=128,'col'=4] {'col'}, dimensions={0}, use_global_device_ids=true | all-gather | bytes 327680 | tf_op jit(solution)/shard_map/all_gather | solution.py:119
  384.2 12.2 %all_gather.93 = f32[512,128]{1,0:T(8,128)S(1)} all-gather(f32[128,128]{1,0:T(8,128)S(1)} %collective-permute-done.24), channel_id=1, replica_groups=mesh['slab'=128,'col'=4] {'col'}, dimensions={0}, use_global_device_ids=true | all-gather | bytes 327680 | tf_op jit(solution)/shard_map/all_gather | solution.py:120
  406.9 12.2 %all_gather.94 = f32[512,128]{1,0:T(8,128)S(1)} all-gather(f32[128,128]{1,0:T(8,128)S(1)} %collective-permute-done.25), channel_id=1, replica_groups=mesh['slab'=128,'col'=4] {'col'}, dimensions={0}, use_global_device_ids=true | all-gather | bytes 327680 | tf_op jit(solution)/shard_map/all_gather | solution.py:119
  419.1 12.2 %all_gather.95 = f32[512,128]{1,0:T(8,128)S(1)} all-gather(f32[128,128]{1,0:T(8,128)S(1)} %collective-permute-done.26), channel_id=1, replica_groups=mesh['slab'=128,'col'=4] {'col'}, dimensions={0}, use_global_device_ids=true | all-gather | bytes 327680 | tf_op jit(solution)/shard_map/all_gather | solution.py:120
  453.1 12.2 %all_gather.97 = f32[512,128]{1,0:T(8,128)S(1)} all-gather(f32[128,128]{1,0:T(8,128)S(1)} %collective-permute-done.28), channel_id=1, replica_groups=mesh['slab'=128,'col'=4] {'col'}, dimensions={0}, use_global_device_ids=true | all-gather | bytes 327680 | tf_op jit(solution)/shard_map/all_gather | solution.py:120
  474.3 12.3 %all_gather.98 = f32[512,128]{1,0:T(8,128)S(1)} all-gather(f32[128,128]{1,0:T(8,128)S(1)} %collective-permute-done.29), channel_id=1, replica_groups=mesh['slab'=128,'col'=4] {'col'}, dimensions={0}, use_global_device_ids=true | all-gather | bytes 327680 | tf_op jit(solution)/shard_map/all_gather | solution.py:119
  486.5 12.2 %all_gather.99 = f32[512,128]{1,0:T(8,128)S(1)} all-gather(f32[128,128]{1,0:T(8,128)S(1)} %collective-permute-done.30), channel_id=1, replica_groups=mesh['slab'=128,'col'=4] {'col'}, dimensions={0}, use_global_device_ids=true | all-gather | bytes 327680 | tf_op jit(solution)/shard_map/all_gather | solution.py:120
  (174 shorter events, 207.9 us)
Async XLA Ops:
  1.0 28.5 %collective-permute-start = (f32[128,128]{0,1:T(8,128)S(1)}, f32[128,128]{0,1:T(8,128)S(1)}, u32[]{:S(2)}, u32[]{:S(2)}) collective-permute-start(f32[128,128]{0,1:T(8,128)S(1)} %bitcast.353), channel_id=1, source_target_pairs={{4,0},{8,4},{12,8},{16,12},{20,16},{24,20},{28,24},{32,28},{36,32}... | collective-permute-start | bytes 196616 | tf_op jit(solution)/shard_map/ppermute | solution.py:13
  11.3 30.7 %collective-permute-start.2 = (f32[128,128]{0,1:T(8,128)S(1)}, f32[128,128]{0,1:T(8,128)S(1)}, u32[]{:S(2)}, u32[]{:S(2)}) collective-permute-start(f32[128,128]{0,1:T(8,128)S(1)} %bitcast.354), channel_id=1, source_target_pairs={{0,4},{4,8},{8,12},{12,16},{16,20},{20,24},{24,28},{28,32},{32,36}... | collective-permute-start | bytes 196616 | tf_op jit(solution)/shard_map/ppermute | solution.py:13
  14.3 39.9 %collective-permute-start.1 = (f32[128,512]{0,1:T(8,128)S(1)}, f32[128,512]{0,1:T(8,128)}, u32[]{:S(2)}, u32[]{:S(2)}) collective-permute-start(f32[128,512]{0,1:T(8,128)S(1)} %bitcast.352), channel_id=1, source_target_pairs={{0,4},{4,8},{8,12},{12,16},{16,20},{20,24},{24,28},{28,32},{32,36}... | collective-permute-start | bytes 786440 | tf_op jit(solution)/shard_map/ppermute | solution.py:13
  54.2 10.5 %all-to-all-start = ((f32[128,4,128]{0,2,1:T(8,128)}), f32[128,4,128]{0,2,1:T(8,128)S(1)}, u32[]{:S(2)}, u32[]{:S(2)}) async-start(f32[128,4,128]{0,2,1:T(8,128)} %bitcast.79), calls=%async_computation | async-start | bytes 524288 | tf_op jit(solution)/shard_map/all_to_all | solution.py:65
  79.9 10.0 %collective-permute-start.4 = (f32[128,128]{0,1:T(8,128)S(1)}, f32[128,128]{0,1:T(8,128)S(1)}, u32[]{:S(2)}, u32[]{:S(2)}) collective-permute-start(f32[128,128]{0,1:T(8,128)S(1)} %copy.494), channel_id=1, source_target_pairs={{0,4},{4,8},{8,12},{12,16},{16,20},{20,24},{24,28},{28,32},{32,36}... | collective-permute-start | bytes 196616 | tf_op jit(solution)/shard_map/ppermute | solution.py:13
  102.4 8.4 %collective-permute-start.5 = (f32[128,128]{0,1:T(8,128)S(1)}, f32[128,128]{0,1:T(8,128)S(1)}, u32[]{:S(2)}, u32[]{:S(2)}) collective-permute-start(f32[128,128]{0,1:T(8,128)S(1)} %copy.496), channel_id=1, source_target_pairs={{8,0},{12,4},{16,8},{20,12},{24,16},{28,20},{32,24},{36,28},{40,32... | collective-permute-start | bytes 196616 | tf_op jit(solution)/shard_map/ppermute | solution.py:13
  108.8 9.5 %collective-permute-start.6 = (f32[128,128]{0,1:T(8,128)S(1)}, f32[128,128]{0,1:T(8,128)S(1)}, u32[]{:S(2)}, u32[]{:S(2)}) collective-permute-start(f32[128,128]{0,1:T(8,128)S(1)} %copy.497), channel_id=1, source_target_pairs={{0,8},{4,12},{8,16},{12,20},{16,24},{20,28},{24,32},{28,36},{32,40... | collective-permute-start | bytes 196616 | tf_op jit(solution)/shard_map/ppermute | solution.py:13
  132.7 10.7 %collective-permute-start.8 = (f32[128,128]{0,1:T(8,128)S(1)}, f32[128,128]{0,1:T(8,128)S(1)}, u32[]{:S(2)}, u32[]{:S(2)}) collective-permute-start(f32[128,128]{0,1:T(8,128)S(1)} %copy.500), channel_id=1, source_target_pairs={{0,16},{4,20},{8,24},{12,28},{16,32},{20,36},{24,40},{28,44},{32,4... | collective-permute-start | bytes 196616 | tf_op jit(solution)/shard_map/ppermute | solution.py:13
  156.0 12.2 %collective-permute-start.10 = (f32[128,128]{0,1:T(8,128)S(1)}, f32[128,128]{0,1:T(8,128)S(1)}, u32[]{:S(2)}, u32[]{:S(2)}) collective-permute-start(f32[128,128]{0,1:T(8,128)S(1)} %copy.503), channel_id=1, source_target_pairs={{0,32},{4,36},{8,40},{12,44},{16,48},{20,52},{24,56},{28,60},{32,6... | collective-permute-start | bytes 196616 | tf_op jit(solution)/shard_map/ppermute | solution.py:13
  160.6 10.3 %collective-permute-start.9 = (f32[128,128]{0,1:T(8,128)S(1)}, f32[128,128]{0,1:T(8,128)S(1)}, u32[]{:S(2)}, u32[]{:S(2)}) collective-permute-start(f32[128,128]{0,1:T(8,128)S(1)} %copy.502), channel_id=1, source_target_pairs={{32,0},{36,4},{40,8},{44,12},{48,16},{52,20},{56,24},{60,28},{64,3... | collective-permute-start | bytes 196616 | tf_op jit(solution)/shard_map/ppermute | solution.py:13
  210.6 8.3 %collective-permute-start.14 = (f32[128,128]{0,1:T(8,128)S(1)}, f32[128,128]{0,1:T(8,128)S(1)}, u32[]{:S(2)}, u32[]{:S(2)}) collective-permute-start(f32[128,128]{0,1:T(8,128)S(1)} %copy.509), channel_id=1, source_target_pairs={{0,128},{4,132},{8,136},{12,140},{16,144},{20,148},{24,152},{28,15... | collective-permute-start | bytes 196616 | tf_op jit(solution)/shard_map/ppermute | solution.py:13
  235.5 10.1 %collective-permute-start.16 = (f32[128,128]{0,1:T(8,128)S(1)}, f32[128,128]{0,1:T(8,128)S(1)}, u32[]{:S(2)}, u32[]{:S(2)}) collective-permute-start(f32[128,128]{0,1:T(8,128)S(1)} %copy.512), channel_id=1, source_target_pairs={{0,256},{4,260},{8,264},{12,268},{16,272},{20,276},{24,280},{28,28... | collective-permute-start | bytes 196616 | tf_op jit(solution)/shard_map/ppermute | solution.py:13
  257.9 10.2 %collective-permute-start.17 = (f32[128,128]{1,0:T(8,128)S(1)}, f32[128,128]{1,0:T(8,128)S(1)}, u32[]{:S(2)}, u32[]{:S(2)}) collective-permute-start(f32[128,128]{1,0:T(8,128)S(1)} %get-tuple-element.366), channel_id=1, source_target_pairs={{0,256},{4,260},{8,264},{12,268},{16,272},{20,276},{24,280},{28,28... | collective-permute-start | bytes 196616 | tf_op jit(solution)/shard_map/ppermute | solution.py:13
  259.4 21.0 %collective-permute-start.18 = (f32[128,128]{1,0:T(8,128)S(1)}, f32[128,128]{1,0:T(8,128)S(1)}, u32[]{:S(2)}, u32[]{:S(2)}) collective-permute-start(f32[128,128]{1,0:T(8,128)S(1)} %get-tuple-element.366), channel_id=1, source_target_pairs={{256,0},{260,4},{264,8},{268,12},{272,16},{276,20},{280,24},{284,2... | collective-permute-start | bytes 196616 | tf_op jit(solution)/shard_map/ppermute | solution.py:13
  296.7 18.6 %collective-permute-start.20 = (f32[128,128]{1,0:T(8,128)S(1)}, f32[128,128]{1,0:T(8,128)S(1)}, u32[]{:S(2)}, u32[]{:S(2)}) collective-permute-start(f32[128,128]{1,0:T(8,128)S(1)} %get-tuple-element.593), channel_id=1, source_target_pairs={{128,0},{132,4},{136,8},{140,12},{144,16},{148,20},{152,24},{156,2... | collective-permute-start | bytes 196616 | tf_op jit(solution)/shard_map/ppermute | solution.py:13
  329.4 17.7 %collective-permute-start.22 = (f32[128,128]{1,0:T(8,128)S(1)}, f32[128,128]{1,0:T(8,128)S(1)}, u32[]{:S(2)}, u32[]{:S(2)}) collective-permute-start(f32[128,128]{1,0:T(8,128)S(1)} %get-tuple-element.594), channel_id=1, source_target_pairs={{64,0},{68,4},{72,8},{76,12},{80,16},{84,20},{88,24},{92,28},{96,3... | collective-permute-start | bytes 196616 | tf_op jit(solution)/shard_map/ppermute | solution.py:13
  359.7 12.2 %collective-permute-start.23 = (f32[128,128]{1,0:T(8,128)S(1)}, f32[128,128]{1,0:T(8,128)S(1)}, u32[]{:S(2)}, u32[]{:S(2)}) collective-permute-start(f32[128,128]{1,0:T(8,128)S(1)} %get-tuple-element.595), channel_id=1, source_target_pairs={{0,32},{4,36},{8,40},{12,44},{16,48},{20,52},{24,56},{28,60},{32,6... | collective-permute-start | bytes 196616 | tf_op jit(solution)/shard_map/ppermute | solution.py:13
  362.2 22.1 %collective-permute-start.24 = (f32[128,128]{1,0:T(8,128)S(1)}, f32[128,128]{1,0:T(8,128)S(1)}, u32[]{:S(2)}, u32[]{:S(2)}) collective-permute-start(f32[128,128]{1,0:T(8,128)S(1)} %get-tuple-element.595), channel_id=1, source_target_pairs={{32,0},{36,4},{40,8},{44,12},{48,16},{52,20},{56,24},{60,28},{64,3... | collective-permute-start | bytes 196616 | tf_op jit(solution)/shard_map/ppermute | solution.py:13
  396.5 10.4 %collective-permute-start.25 = (f32[128,128]{1,0:T(8,128)S(1)}, f32[128,128]{1,0:T(8,128)S(1)}, u32[]{:S(2)}, u32[]{:S(2)}) collective-permute-start(f32[128,128]{1,0:T(8,128)S(1)} %get-tuple-element.596), channel_id=1, source_target_pairs={{0,16},{4,20},{8,24},{12,28},{16,32},{20,36},{24,40},{28,44},{32,4... | collective-permute-start | bytes 196616 | tf_op jit(solution)/shard_map/ppermute | solution.py:13
  398.4 20.7 %collective-permute-start.26 = (f32[128,128]{1,0:T(8,128)S(1)}, f32[128,128]{1,0:T(8,128)S(1)}, u32[]{:S(2)}, u32[]{:S(2)}) collective-permute-start(f32[128,128]{1,0:T(8,128)S(1)} %get-tuple-element.596), channel_id=1, source_target_pairs={{16,0},{20,4},{24,8},{28,12},{32,16},{36,20},{40,24},{44,28},{48,3... | collective-permute-start | bytes 196616 | tf_op jit(solution)/shard_map/ppermute | solution.py:13
  431.4 9.5 %collective-permute-start.27 = (f32[128,128]{1,0:T(8,128)S(1)}, f32[128,128]{1,0:T(8,128)S(1)}, u32[]{:S(2)}, u32[]{:S(2)}) collective-permute-start(f32[128,128]{1,0:T(8,128)S(1)} %get-tuple-element.597), channel_id=1, source_target_pairs={{0,8},{4,12},{8,16},{12,20},{16,24},{20,28},{24,32},{28,36},{32,40... | collective-permute-start | bytes 196616 | tf_op jit(solution)/shard_map/ppermute | solution.py:13
  433.3 19.8 %collective-permute-start.28 = (f32[128,128]{1,0:T(8,128)S(1)}, f32[128,128]{1,0:T(8,128)S(1)}, u32[]{:S(2)}, u32[]{:S(2)}) collective-permute-start(f32[128,128]{1,0:T(8,128)S(1)} %get-tuple-element.597), channel_id=1, source_target_pairs={{8,0},{12,4},{16,8},{20,12},{24,16},{28,20},{32,24},{36,28},{40,32... | collective-permute-start | bytes 196616 | tf_op jit(solution)/shard_map/ppermute | solution.py:13
  465.3 8.9 %collective-permute-start.29 = (f32[128,128]{1,0:T(8,128)S(1)}, f32[128,128]{1,0:T(8,128)S(1)}, u32[]{:S(2)}, u32[]{:S(2)}) collective-permute-start(f32[128,128]{1,0:T(8,128)S(1)} %get-tuple-element.598), channel_id=1, source_target_pairs={{0,4},{4,8},{8,12},{12,16},{16,20},{20,24},{24,28},{28,32},{32,36}... | collective-permute-start | bytes 196616 | tf_op jit(solution)/shard_map/ppermute | solution.py:13
  467.3 19.2 %collective-permute-start.30 = (f32[128,128]{1,0:T(8,128)S(1)}, f32[128,128]{1,0:T(8,128)S(1)}, u32[]{:S(2)}, u32[]{:S(2)}) collective-permute-start(f32[128,128]{1,0:T(8,128)S(1)} %get-tuple-element.598), channel_id=1, source_target_pairs={{4,0},{8,4},{12,8},{16,12},{20,16},{24,20},{28,24},{32,28},{36,32}... | collective-permute-start | bytes 196616 | tf_op jit(solution)/shard_map/ppermute | solution.py:13
  (17 other events, 195.6 us)
where the time goes:
time: 501 us; the launch traced here: 499 us
  blocking collectives  308 us (61%)
  starting transfers between devices  130 us (26%)
  waiting for transfers between devices  50.1 us (10%)
  matrix products  5.2 us (1%)
  local copies, waits for them, and re-layouts  5.04 us (1%)
    ppermute x31, starting transfers between devices, from_behind(): return lax.ppermute(block, axis, route)  126 us
    all_gather x8, blocking collectives, gather_rows(): return lax.all_gather(values, 'col', axis=0, tiled=True)  98.5 us
    all_gather x7, blocking collectives, per_device(): lax.all_gather(upper_in, 'col', axis=0, tiled=True)  86 us
    all_gather x7, blocking collectives, per_device(): lax.all_gather(lower_in, 'col', axis=0, tiled=True)  85.9 us
    ppermute x31, waiting for transfers between devices, from_behind(): return lax.ppermute(block, axis, route)  43.8 us
    all_gather x1, blocking collectives, per_device(): lax.all_gather(states, 'col', axis=0, tiled=True)  12.6 us
    all_gather x1, blocking collectives, per_device(): lax.all_gather(next_shard, 'col', axis=0, tiled=True)  12.5 us
    all_gather x1, blocking collectives, per_device(): lax.all_gather(prev_shard, 'col', axis=0, tiled=True)  12.2 us
  transfers between devices with their start and end apart: 32, of which 18 were waited for; matrix products, arithmetic and copies ran while one was open for 1% of the time, Pallas kernels for 0%

commit v1 on v0

v1 whole, which is shorter than its diff:
```python
import functools

import jax
import jax.numpy as jnp
from jax import lax
from jax.experimental import pallas as pl
from jax.experimental.pallas import tpu as pltpu
from jax.sharding import PartitionSpec as P

MESH = pl.DeviceIdType.MESH
half_step = 0.5


def rotate(values):
    width = values.shape[-1]
    column = lax.broadcasted_iota(jnp.int32, values.shape, values.ndim - 1)
    return jnp.where(
        column % 2 == 0,
        -pltpu.roll(values, width - 1, values.ndim - 1),
        pltpu.roll(values, 1, values.ndim - 1),
    )


def split(values):
    high = values.astype(jnp.bfloat16)
    low = (values - high.astype(jnp.float32)).astype(jnp.bfloat16)
    return high, low


def split_wide(values):
    return jnp.concatenate(split(values), axis=1)


def three_pass(tall_pair, wide_pair):
    product = jnp.dot(tall_pair, wide_pair, preferred_element_type=jnp.float32)
    rows, columns = product.shape[0] // 2, product.shape[1] // 2
    return product[:rows, :columns] + (product[:rows, columns:] + product[rows:, :columns])


def complex_rows(tall_pair, wide_pair):
    both = three_pass(tall_pair, wide_pair)
    rows = both.shape[0] // 2
    return both[:rows] + rotate(both[rows:])


def kernel(
    slabs,
    levels,
    parts,
    psi_h,
    energy_h,
    tunnel_h,
    pivot_h,
    beneath_reduce_h,
    above_reduce_h,
    beneath_solve_h,
    above_solve_h,
    out,
    psi_full,
    next_full,
    prev_parts,
    prev_send,
    energy_v,
    tunnel_v,
    blocks_v,
    energy_w,
    tunnel_w,
    pivot_w,
    reduce_w,
    solve_w,
    x_full,
    pivot_part,
    reduce_in,
    reduce_out,
    solve_in,
    load_sem,
    psi_send,
    psi_recv,
    next_send,
    next_recv,
    prev_send_sem,
    prev_recv,
    x_send,
    x_recv,
    reduce_send,
    reduce_recv,
    solve_send,
    solve_recv,
):
    s = lax.axis_index("slab")
    c = lax.axis_index("col")
    level = jnp.int32(0)
    reach = jnp.int32(1)
    for k in range(1, levels + 1):
        at_least = s % (2**k) == 0
        level = jnp.where(at_least, k, level)
        reach = jnp.where(at_least, 2**k, reach)
    is_root = s == 0
    partner_levels = jnp.minimum(level + 1, levels)
    rows = psi_h.shape[1]
    depth = parts * rows

    def everyone_of(slab, act):
        for step in (2, 1, 3, 0):
            act((slab, (c + step) % parts))

    def rest_of_row(act):
        for step in (2, 1, 3):
            act((s, (c + step) % parts))

    def load(index, source, target):
        return pltpu.make_async_copy(source, target, load_sem.at[index])

    loads = [
        load(0, psi_h.at[0], psi_full.at[c]),
        load(1, tunnel_h.at[0], tunnel_v),
        load(2, energy_h.at[0], energy_v),
        load(3, beneath_reduce_h.at[0], blocks_v.at[0]),
        load(4, above_reduce_h.at[0], blocks_v.at[1]),
        load(5, pivot_h.at[0], blocks_v.at[2]),
        load(6, beneath_solve_h.at[0], blocks_v.at[3]),
        load(7, above_solve_h.at[0], blocks_v.at[4]),
    ]
    for copy in loads:
        copy.start()

    barrier = pltpu.get_barrier_semaphore()

    def greet(device):
        pl.semaphore_signal(barrier, inc=1, device_id=device, device_id_type=MESH)

    rest_of_row(greet)

    @pl.loop(0, partner_levels)
    def _(j):
        distance = jnp.left_shift(jnp.int32(1), j)

        @pl.when(s - distance >= 0)
        def _():
            everyone_of(s - distance, greet)

        @pl.when(s + distance < slabs)
        def _():
            everyone_of(s + distance, greet)

    has_above = s + reach < slabs
    both_sides = jnp.where(is_root, levels, 2 * level + 1 + has_above.astype(jnp.int32))

    loads[0].wait()
    loads[1].wait()
    own = psi_full[c]
    tunnel = tunnel_v[...]
    prev_send[...] = three_pass(
        jnp.concatenate(split(tunnel.T), axis=0), split_wide(own)
    ).reshape(prev_send.shape)
    tunnel_w[...] = jnp.concatenate(split(tunnel), axis=0)

    pl.semaphore_wait(barrier, (parts - 1) + parts * both_sides)

    def remote(source, target, send, recv, device):
        return pltpu.make_async_remote_copy(
            src_ref=source, dst_ref=target, send_sem=send, recv_sem=recv,
            device_id=device, device_id_type=MESH,
        )

    def send_psi_row():
        rest_of_row(
            lambda device: remote(
                psi_full.at[c], psi_full.at[c], psi_send, psi_recv, device
            ).start()
        )

    def send_next():
        @pl.when(s > 0)
        def _():
            everyone_of(
                s - 1,
                lambda device: remote(
                    psi_full.at[c], next_full.at[c], next_send, next_recv, device
                ).start(),
            )

    def send_prev():
        @pl.when(s + 1 < slabs)
        def _():
            everyone_of(
                s + 1,
                lambda device: remote(
                    prev_send.at[device[1]], prev_parts.at[c], prev_send_sem, prev_recv, device
                ).start(),
            )

    @pl.when(s % 2 == 1)
    def _():
        send_psi_row()
        send_next()
        send_prev()

    @pl.when(s % 2 == 0)
    def _():
        send_next()
        send_prev()
        send_psi_row()

    def stacked(index):
        block = blocks_v[index].reshape(2 * rows, depth)
        return jnp.concatenate(split(block), axis=0)

    loads[2].wait()
    energy_w[...] = jnp.concatenate(split(energy_v[...]), axis=0)
    loads[3].wait()
    reduce_w[0] = stacked(0)
    loads[4].wait()
    reduce_w[1] = stacked(1)

    def arrived(ref, sem):
        pltpu.make_async_copy(ref, ref, sem).wait()

    arrived(psi_full.at[pl.ds(0, parts - 1)], psi_recv)
    x_full[c] = three_pass(energy_w[...], split_wide(psi_full[...].reshape(depth, -1)))

    @pl.when(s + 1 < slabs)
    def _():
        arrived(next_full, next_recv)
        x_full[c] += three_pass(tunnel_w[...], split_wide(next_full[...].reshape(depth, -1)))

    @pl.when(s > 0)
    def _():
        arrived(prev_parts, prev_recv)
        x_full[c] += (prev_parts[0] + prev_parts[1]) + (prev_parts[2] + prev_parts[3])

    x_full[c] = psi_full[c] - half_step * rotate(x_full[c])
    rest_of_row(
        lambda device: remote(x_full.at[c], x_full.at[c], x_send, x_recv, device).start()
    )

    loads[5].wait()
    pivot_w[...] = stacked(2)
    loads[6].wait()
    solve_w[0] = stacked(3)
    loads[7].wait()
    solve_w[1] = stacked(4)

    arrived(x_full.at[pl.ds(0, parts - 1)], x_recv)
    arrived(x_full.at[pl.ds(0, parts - 1)], x_send)

    @pl.loop(0, level)
    def _(j):
        arrived(reduce_in.at[j, 1], reduce_recv.at[j, 1])
        x_full[...] -= reduce_in[j, 1]

        @pl.when(s > 0)
        def _():
            arrived(reduce_in.at[j, 0], reduce_recv.at[j, 0])
            x_full[...] -= reduce_in[j, 0]

    wide = split_wide(x_full[...].reshape(depth, -1))
    odd_pair = (s // reach // 2) % 2

    @pl.when(s > 0)
    def _():
        @pl.loop(0, 2)
        def _(turn):
            side = jnp.where(odd_pair == 1, turn, 1 - turn)
            target = s + (2 * side - 1) * reach

            @pl.when(target < slabs)
            def _():
                reduce_out[side] = complex_rows(reduce_w[side], wide)
                everyone_of(
                    target,
                    lambda device: remote(
                        reduce_out.at[side],
                        reduce_in.at[level, 1 - side, c],
                        reduce_send.at[side],
                        reduce_recv.at[level, 1 - side],
                        device,
                    ).start(),
                )

    pivot_part[...] = complex_rows(pivot_w[...], wide)

    @pl.when(s > 0)
    def _():
        @pl.loop(0, 2)
        def _(turn):
            side = jnp.where(odd_pair == 1, 1 - turn, turn)

            @pl.when(s + (2 * side - 1) * reach < slabs)
            def _():
                arrived(solve_in.at[side], solve_recv.at[side])
                pivot_part[...] -= complex_rows(
                    solve_w[side], split_wide(solve_in[side].reshape(depth, -1))
                )

    def send_solved(j, side):
        target = s + (2 * side - 1) * jnp.left_shift(jnp.int32(1), j)
        everyone_of(
            target,
            lambda device: remote(
                pivot_part,
                solve_in.at[1 - side, c],
                solve_send.at[j, side],
                solve_recv.at[1 - side],
                device,
            ).start(),
        )

    @pl.loop(0, level)
    def _(i):
        j = level - 1 - i
        send_solved(j, 1)

        @pl.when(s > 0)
        def _():
            send_solved(j, 0)

    out[0] = pivot_part[...]

    arrived(psi_full.at[pl.ds(0, parts - 1)], psi_send)

    @pl.when(s > 0)
    def _():
        arrived(next_full, next_send)

    @pl.when(s + 1 < slabs)
    def _():
        arrived(prev_parts, prev_send_sem)

    @pl.when(s > 0)
    def _():
        @pl.loop(0, 2)
        def _(side):
            @pl.when(s + (2 * side - 1) * reach < slabs)
            def _():
                arrived(solve_in.at[side], reduce_send.at[side])

    @pl.loop(0, level)
    def _(j):
        arrived(solve_in.at[1], solve_send.at[j, 1])

        @pl.when(s > 0)
        def _():
            arrived(solve_in.at[0], solve_send.at[j, 0])


def per_device(*args):
    slabs = lax.axis_size("slab")
    levels = slabs.bit_length() - 1
    parts = lax.axis_size("col")
    psi = args[0]
    rows, width = psi.shape[1:]
    depth = parts * rows
    f32, bf16 = jnp.float32, jnp.bfloat16
    gathered = pltpu.VMEM((parts, rows, width), f32)
    dma = pltpu.SemaphoreType.DMA
    return pl.pallas_call(
        functools.partial(kernel, slabs, levels, parts),
        out_shape=jax.ShapeDtypeStruct(psi.shape, psi.dtype),
        in_specs=[pl.BlockSpec(memory_space=pl.ANY)] * len(args),
        out_specs=pl.BlockSpec(memory_space=pltpu.VMEM),
        scratch_shapes=[
            gathered,
            gathered,
            gathered,
            gathered,
            pltpu.VMEM((rows, depth), f32),
            pltpu.VMEM((rows, depth), f32),
            pltpu.VMEM((5, 2, rows, depth), f32),
            pltpu.VMEM((2 * rows, depth), bf16),
            pltpu.VMEM((2 * rows, depth), bf16),
            pltpu.VMEM((4 * rows, depth), bf16),
            pltpu.VMEM((2, 4 * rows, depth), bf16),
            pltpu.VMEM((2, 4 * rows, depth), bf16),
            gathered,
            pltpu.VMEM((rows, width), f32),
            pltpu.VMEM((levels, 2, parts, rows, width), f32),
            pltpu.VMEM((2, rows, width), f32),
            pltpu.VMEM((2, parts, rows, width), f32),
            dma((8,)),
            dma,
            dma,
            dma,
            dma,
            dma,
            dma,
            dma,
            dma,
            dma((2,)),
            dma((levels, 2)),
            dma((levels, 2)),
            dma((2,)),
        ],
        compiler_params=pltpu.CompilerParams(
            collective_id=0, has_side_effects=True, vmem_limit_bytes=40 * 2**20
        ),
    )(*args)


def solution(mesh):
    vector = P("slab", "col", None)
    block = P("slab", None, "col", None)
    return jax.shard_map(
        per_device,
        mesh=mesh,
        in_specs=(vector,) * 3 + (block,) * 5,
        out_specs=vector,
        check_vma=False,
    )
```

time: 501 us -> 136 us (0.27)
  the two profiles are of different devices: /device:TPU:32 before, /device:TPU:1 now
where the time goes in v1:
time: 136 us
  Pallas kernels  127 us (93%)
  local copies, waits for them, and re-layouts  8.58 us (6%)
    pallas_call x1, Pallas kernels, per_device(): pl.pallas_call(functools.partial(kernel, slabs, levels, parts), out_shape...  127 us
    unnamed x17, local copies, waits for them, and re-layouts  8.58 us

profile of v1, /device:TPU:1, one launch (start us, length us, event | category | flops | bytes accessed | tf_op | source)
XLA Modules:
  0.0 135.6 jit_solution(4234846961666663830)
XLA Ops:
  0.0 0.0 copy-start
  0.0 1.0 copy-done
  1.0 0.0 copy-start.1
  1.0 1.0 copy-done.1
  2.1 0.0 copy-start.2
  2.1 1.0 copy-done.2
  3.1 0.0 copy-start.3
  3.1 1.0 copy-done.3
  4.2 0.0 copy-start.4
  4.2 1.0 copy-done.4
  5.2 0.0 copy-start.5
  5.2 0.9 copy-done.5
  6.2 0.0 copy-start.6
  6.2 0.9 copy-done.6
  7.1 0.0 copy-start.7
  7.1 0.8 copy-done.7
  8.0 127.0 %shard_map.82 = f32[1,128,128]{2,1,0:T(8,128)S(1)} custom-call(f32[1,128,128]{2,1,0:T(8,128)S(1)} %copy-done.7, f32[1,128,512]{2,1,0:T(8,128)S(1)} %copy-done.5, f32[1,128,512]{2,1,0:T(8,128)S(1)} %copy-done.6, f32[1,2,128,512]{3,2,1,0:T(8,128)S(1)} %copy-done, f32[1,2,128,512]{3,2,1,0:T(8,128)S(1)} %copy-done.1, f32[1,2,128,512]{3,2,1,0:T(8,128)S(1)} %copy-done.2, ...), custom_call_target="tpu_custom_call" | custom-call | tf_op jit(solution)/shard_map/pallas_call | solution.py:357
  135.0 0.6 copy.10
Async XLA Ops:
  0.0 1.0 copy-start
  1.0 1.0 copy-start.1
  2.1 1.0 copy-start.2
  3.1 1.0 copy-start.3
  4.2 1.0 copy-start.4
  5.2 0.9 copy-start.5
  6.2 0.9 copy-start.6
  7.1 0.8 copy-start.7

commit v2 on v1

--- a/solution.py
+++ b/solution.py
@@ -190,13 +190,13 @@
                 ).start(),
             )
 
-    @pl.when(s % 2 == 1)
+    odd = s % 2 == 1
+
+    @pl.when(odd)
     def _():
         send_psi_row()
-        send_next()
-        send_prev()
-
-    @pl.when(s % 2 == 0)
+
+    @pl.when(jnp.logical_not(odd))
     def _():
         send_next()
         send_prev()
@@ -233,6 +233,11 @@
     rest_of_row(
         lambda device: remote(x_full.at[c], x_full.at[c], x_send, x_recv, device).start()
     )
+
+    @pl.when(odd)
+    def _():
+        remote(psi_full, next_full, next_send, next_recv, (s - 1, c)).start()
+        send_prev()
 
     loads[5].wait()
     pivot_w[...] = stacked(2)
@@ -357,7 +362,7 @@
     return pl.pallas_call(
         functools.partial(kernel, slabs, levels, parts),
         out_shape=jax.ShapeDtypeStruct(psi.shape, psi.dtype),
-        in_specs=[pl.BlockSpec(memory_space=pl.ANY)] * len(args),
+        in_specs=[pl.BlockSpec(memory_space=pltpu.HBM)] * len(args),
         out_specs=pl.BlockSpec(memory_space=pltpu.VMEM),
         scratch_shapes=[
             gathered,

time: 136 us -> 137 us (level)
  no operation moved by 1% of the time
where the time goes in v2:
time: 137 us; the launch traced here: 136 us
  Pallas kernels  127 us (93%)
  local copies, waits for them, and re-layouts  8.58 us (6%)
    pallas_call x1, Pallas kernels, per_device(): pl.pallas_call(functools.partial(kernel, slabs, levels, parts), out_shape...  127 us
    unnamed x17, local copies, waits for them, and re-layouts  8.58 us

profile of v2, /device:TPU:1, one launch (start us, length us, event | category | flops | bytes accessed | tf_op | source)
XLA Modules:
  0.0 136.1 jit_solution(2700039859470705453)
XLA Ops:
  0.0 0.0 copy-start
  0.0 1.0 copy-done
  1.0 0.0 copy-start.1
  1.0 1.0 copy-done.1
  2.1 0.0 copy-start.2
  2.1 1.0 copy-done.2
  3.1 0.0 copy-start.3
  3.1 1.0 copy-done.3
  4.2 0.0 copy-start.4
  4.2 1.0 copy-done.4
  5.2 0.0 copy-start.5
  5.2 0.9 copy-done.5
  6.2 0.0 copy-start.6
  6.2 0.9 copy-done.6
  7.1 0.0 copy-start.7
  7.1 0.8 copy-done.7
  8.0 127.5 %shard_map.82 = f32[1,128,128]{2,1,0:T(8,128)S(1)} custom-call(f32[1,128,128]{2,1,0:T(8,128)S(1)} %copy-done.7, f32[1,128,512]{2,1,0:T(8,128)S(1)} %copy-done.5, f32[1,128,512]{2,1,0:T(8,128)S(1)} %copy-done.6, f32[1,2,128,512]{3,2,1,0:T(8,128)S(1)} %copy-done, f32[1,2,128,512]{3,2,1,0:T(8,128)S(1)} %copy-done.1, f32[1,2,128,512]{3,2,1,0:T(8,128)S(1)} %copy-done.2, ...), custom_call_target="tpu_custom_call" | custom-call | tf_op jit(solution)/shard_map/pallas_call | solution.py:362
  135.4 0.6 copy.10
Async XLA Ops:
  0.0 1.0 copy-start
  1.0 1.0 copy-start.1
  2.1 1.0 copy-start.2
  3.1 1.0 copy-start.3
  4.2 1.0 copy-start.4
  5.2 0.9 copy-start.5
  6.2 0.9 copy-start.6
  7.1 0.8 copy-start.7

commit v3 on v2

--- a/solution.py
+++ b/solution.py
@@ -397,7 +397,7 @@
             dma((2,)),
         ],
         compiler_params=pltpu.CompilerParams(
-            collective_id=0, has_side_effects=True, vmem_limit_bytes=40 * 2**20
+            collective_id=0, has_side_effects=True, vmem_limit_bytes=56 * 2**20
         ),
     )(*args)
 

time: 137 us -> 129 us (0.942)
  local copies, waits for them, and re-layouts: 8.58 us -> 1.47 us
    unnamed x17 -> x1, local copies, waits for them, and re-layouts: 8.58 us -> 1.47 us
where the time goes in v3:
time: 129 us
  Pallas kernels  128 us (99%)
  local copies, waits for them, and re-layouts  1.47 us (1%)
    pallas_call x1, Pallas kernels, per_device(): pl.pallas_call(functools.partial(kernel, slabs, levels, parts), out_shape...  128 us

profile of v3, /device:TPU:1, one launch (start us, length us, event | category | flops | bytes accessed | tf_op | source)
XLA Modules:
  0.0 129.3 jit_solution(8797251944884646714)
XLA Ops:
  0.0 127.8 %shard_map.82 = f32[1,128,128]{2,1,0:T(8,128)} custom-call(f32[1,128,128]{2,1,0:T(8,128)} %psi_h.1, f32[1,128,512]{2,1,0:T(8,128)} %energy_h.1, f32[1,128,512]{2,1,0:T(8,128)} %tunnel_h.1, f32[1,2,128,512]{3,2,1,0:T(8,128)} %pivot_h.1, f32[1,2,128,512]{3,2,1,0:T(8,128)} %beneath_reduce_h.1, f32[1,2,128,512]{3,2,1,0:T(8,128)} %above_reduce_h.1, ...), custom_call_target="tpu_custom_call" | custom-call | tf_op jit(solution)/shard_map/pallas_call | solution.py:362
  127.8 1.5 %copy.10 = f32[1,128,128]{2,1,0:T(8,128)} copy(f32[1,128,128]{2,1,0:T(8,128)} %shard_map.82) | data formatting | bytes 131072

commit v4 on v0

v4 whole, which is shorter than its diff:
```python
import functools

import jax
import jax.numpy as jnp
from jax import lax
from jax.experimental import pallas as pl
from jax.experimental.pallas import tpu as pltpu
from jax.sharding import PartitionSpec as P

MESH = pl.DeviceIdType.MESH
half_step = 0.5
ROW_LEVELS = 2
BENEATH_R, ABOVE_R, PIVOT, BENEATH_S, ABOVE_S = range(5)


def rotate(values):
    height = values.shape[0]
    row = lax.broadcasted_iota(jnp.int32, values.shape, 0)
    return jnp.where(
        row % 2 == 0, -pltpu.roll(values, height - 1, 0), pltpu.roll(values, 1, 0)
    )


def split(values):
    high = values.astype(jnp.bfloat16)
    low = (values - high.astype(jnp.float32)).astype(jnp.bfloat16)
    return high, low


def split_tall(values):
    return jnp.concatenate(split(values), axis=0)


def fold(product):
    m, n = product.shape[0] // 2, product.shape[1] // 2
    return product[:m, :n] + (product[m:, :n] + product[:m, n:])


def times_rows(tall, block_rows):
    return fold(
        lax.dot_general(
            tall, block_rows, (((1,), (1,)), ((), ())), preferred_element_type=jnp.float32
        )
    )


def times_columns(tall, block_columns):
    return fold(jnp.dot(tall, block_columns, preferred_element_type=jnp.float32))


def join(both):
    n = both.shape[1] // 2
    return both[:, :n] + rotate(both[:, n:])


def side_by_side(pieces):
    return jnp.concatenate([pieces[k] for k in range(pieces.shape[0])], axis=1)


def place_of(slab, levels):
    level, reach = jnp.int32(0), jnp.int32(1)
    for k in range(1, levels + 1):
        at_least = slab % (2**k) == 0
        level = jnp.where(at_least, k, level)
        reach = jnp.where(at_least, 2**k, reach)
    return level, reach


def kernel(slabs, levels, parts, *refs):
    (
        psi_h, energy_h, tunnel_h, pivot_h, beneath_reduce_h, above_reduce_h,
        beneath_solve_h, above_solve_h, out,
        psi_raw, energy_v, tunnel_v, blocks_v, turned_v,
        psi_full, next_full, prev_parts, prev_send_v, x_full,
        energy_w, tunnel_w, own_w, row_raw, row_w, state_raw, state_w,
        pivot_odd, odd_out,
        rhs_row, row_in, row_x, row_out,
        rhs_state, state_in, state_x, state_out,
        solve_in, solved, odd_in, out_in,
        load_sem, psi_send, psi_recv, next_send, next_recv, prev_send, prev_recv,
        x_send, x_recv, rhs_send, rhs_recv, mat_send, mat_recv, odd_send, up_send,
        reduce_recv, solve_send, solve_recv, last_send, last_recv, out_send, out_recv, go,
    ) = refs
    s = lax.axis_index("slab")
    c = lax.axis_index("col")
    odd = s % 2 == 1
    even = s % 2 == 0
    chip = s // 2
    e = chip * 2
    level, reach = place_of(e, levels)
    level_next, _ = place_of(e + 2, levels)
    is_root = e == 0
    not_root = e > 0
    state_role = level > ROW_LEVELS
    row_role = level <= ROW_LEVELS
    has_next = e + 2 < slabs
    rows, width = psi_h.shape[1:]
    depth = parts * rows
    quarter = width // parts

    def around(slab, act, skip_own=False):
        for step in (2, 1, 3) if skip_own else (2, 1, 3, 0):
            act((slab, (c + step) % parts))

    def arrived(ref, sem):
        pltpu.make_async_copy(ref, ref, sem).wait()

    def send(source, target, send_sem, recv_sem, device):
        pltpu.make_async_remote_copy(
            src_ref=source, dst_ref=target, send_sem=send_sem, recv_sem=recv_sem,
            device_id=device, device_id_type=MESH,
        ).start()

    def states_of(col):
        return pl.ds(pl.multiple_of(col * quarter, quarter), quarter)

    def load(index, source, target):
        return pltpu.make_async_copy(source, target, load_sem.at[index])

    loads = [
        load(0, psi_h.at[0], psi_raw),
        load(1, tunnel_h.at[0], tunnel_v),
        load(2, energy_h.at[0], energy_v),
        load(3, beneath_reduce_h.at[0], blocks_v.at[BENEATH_R]),
        load(4, above_reduce_h.at[0], blocks_v.at[ABOVE_R]),
        load(5, pivot_h.at[0], blocks_v.at[PIVOT]),
        load(6, beneath_solve_h.at[0], blocks_v.at[BENEATH_S]),
        load(7, above_solve_h.at[0], blocks_v.at[ABOVE_S]),
    ]
    for copy in loads:
        copy.start()

    barrier = pltpu.get_barrier_semaphore()

    def greet(device):
        pl.semaphore_signal(barrier, inc=1, device_id=device, device_id_type=MESH)

    around(s, greet, skip_own=True)
    around(s + 1 - 2 * (s % 2), greet)
    expected = jnp.int32(2 * parts - 1)

    @pl.when(jnp.logical_and(even, not_root))
    def _():
        around(s - 1, greet)

    @pl.when(jnp.logical_and(odd, has_next))
    def _():
        around(s + 1, greet)

    expected += parts * jnp.where(odd, has_next, not_root).astype(jnp.int32)
    for j in range(1, levels):
        for sign in (-1, 1):
            target = s + sign * 2**j
            there = jnp.logical_and(target >= 0, target < slabs)
            if j > 1:
                there = jnp.logical_and(there, j <= level)
            there = jnp.logical_and(there, odd)
            count = parts if j <= max(ROW_LEVELS, 1) else 1
            expected += count * there.astype(jnp.int32)

            @pl.when(there)
            def _():
                if count > 1:
                    around(target, greet)
                else:
                    greet((target, c))

    loads[0].wait()
    loads[1].wait()
    own = psi_raw[...].T
    psi_full[c] = own
    tunnel = tunnel_v[...]
    wide_tunnel = jnp.concatenate(split(tunnel), axis=1)
    partial = times_columns(split_tall(own), wide_tunnel)
    for k in range(parts):
        prev_send_v[k] = partial[:, k * rows : (k + 1) * rows]

    pl.semaphore_wait(barrier, expected)

    def send_psi_row():
        around(
            s,
            lambda device: send(psi_full.at[c], psi_full.at[c], psi_send, psi_recv, device),
            skip_own=True,
        )

    def send_prev():
        around(
            s + 1,
            lambda device: send(
                prev_send_v.at[device[1]], prev_parts.at[c], prev_send, prev_recv, device
            ),
        )

    @pl.when(odd)
    def _():
        send_psi_row()

    @pl.when(even)
    def _():
        @pl.when(not_root)
        def _():
            around(
                s - 1,
                lambda device: send(
                    psi_full.at[c], next_full.at[c], next_send, next_recv, device
                ),
            )

        send_prev()
        send_psi_row()

    def stacked(block):
        return split_tall(block.reshape(2 * rows, depth))

    tunnel_w[...] = split_tall(tunnel)
    loads[2].wait()
    energy_w[...] = split_tall(energy_v[...])
    for index in range(5):
        loads[3 + index].wait()

    def turn(index):
        for part in range(2):
            turned_v[index, part] = blocks_v[index, part].T

    def pass_on(index):
        around(
            s + 1,
            lambda device: send(
                turned_v.at[index],
                state_raw.at[index, c],
                mat_send.at[index],
                mat_recv.at[index],
                device,
            ),
        )

    @pl.when(even)
    def _():
        @pl.when(row_role)
        def _():
            for index in (BENEATH_R, ABOVE_R):
                send(
                    blocks_v.at[index], row_raw.at[index], mat_send.at[index],
                    mat_recv.at[index], (s + 1, c),
                )

        @pl.when(jnp.logical_and(state_role, not_root))
        def _():
            for index in (BENEATH_R, ABOVE_R):
                turn(index)
                pass_on(index)

    @pl.when(odd)
    def _():
        own_w[BENEATH_R] = stacked(blocks_v[BENEATH_R])
        own_w[ABOVE_R] = stacked(blocks_v[ABOVE_R])

    arrived(psi_full.at[pl.ds(0, parts - 1)], psi_recv)
    x_full[c] = times_rows(split_tall(side_by_side(psi_full[...])), energy_w[...])

    @pl.when(s > 0)
    def _():
        arrived(prev_parts, prev_recv)
        x_full[c] += (prev_parts[0] + prev_parts[1]) + (prev_parts[2] + prev_parts[3])

    @pl.when(s + 1 < slabs)
    def _():
        arrived(next_full, next_recv)
        x_full[c] += times_rows(split_tall(side_by_side(next_full[...])), tunnel_w[...])

    x_full[c] = psi_full[c] - half_step * rotate(x_full[c])

    @pl.when(even)
    def _():
        @pl.when(state_role)
        def _():
            around(
                s + 1,
                lambda device: send(
                    x_full.at[c, states_of(device[1])], rhs_state.at[c], rhs_send, rhs_recv, device
                ),
            )

        @pl.when(row_role)
        def _():
            around(
                s + 1,
                lambda device: send(x_full.at[c], rhs_row.at[c], rhs_send, rhs_recv, device),
            )

        turn(PIVOT)

        @pl.when(not_root)
        def _():
            turn(BENEATH_S)
            turn(ABOVE_S)

        pl.semaphore_wait(go, 1)
        pass_on(PIVOT)

        @pl.when(not_root)
        def _():
            pass_on(BENEATH_S)
            pass_on(ABOVE_S)

        arrived(out_in, out_recv)
        out[0] = out_in[...].T

        arrived(psi_full.at[pl.ds(0, parts - 1)], psi_send)
        arrived(prev_parts, prev_send)

        @pl.when(not_root)
        def _():
            arrived(next_full, next_send)
            arrived(state_raw.at[BENEATH_S], mat_send.at[BENEATH_S])
            arrived(state_raw.at[ABOVE_S], mat_send.at[ABOVE_S])

            @pl.when(state_role)
            def _():
                arrived(state_raw.at[BENEATH_R], mat_send.at[BENEATH_R])
                arrived(state_raw.at[ABOVE_R], mat_send.at[ABOVE_R])

        arrived(state_raw.at[PIVOT], mat_send.at[PIVOT])

        @pl.when(state_role)
        def _():
            arrived(rhs_state, rhs_send)

        @pl.when(row_role)
        def _():
            arrived(rhs_row, rhs_send)
            arrived(row_raw.at[BENEATH_R], mat_send.at[BENEATH_R])
            arrived(row_raw.at[ABOVE_R], mat_send.at[ABOVE_R])

    @pl.when(odd)
    def _():
        around(
            s,
            lambda device: send(x_full.at[c], x_full.at[c], x_send, x_recv, device),
            skip_own=True,
        )
        send(psi_full, next_full, next_send, next_recv, (s - 1, c))

        @pl.when(has_next)
        def _():
            send_prev()

        own_w[PIVOT] = stacked(blocks_v[PIVOT])
        own_w[BENEATH_S] = stacked(blocks_v[BENEATH_S])
        own_w[ABOVE_S] = stacked(blocks_v[ABOVE_S])

        arrived(x_full.at[pl.ds(0, parts - 1)], x_recv)
        tall = split_tall(side_by_side(x_full[...]))

        def send_rows(source, host, to_state, tier, side, sem, skip_own=False):
            @pl.when(to_state)
            def _():
                around(
                    host,
                    lambda device: send(
                        source.at[states_of(device[1])],
                        state_in.at[tier, side, c],
                        sem,
                        reduce_recv.at[tier, side],
                        device,
                    ),
                    skip_own,
                )

            @pl.when(jnp.logical_not(to_state))
            def _():
                around(
                    host,
                    lambda device: send(
                        source,
                        row_in.at[jnp.minimum(tier, ROW_LEVELS - 1), side, c],
                        sem,
                        reduce_recv.at[tier, side],
                        device,
                    ),
                    skip_own,
                )

        def odd_beneath():
            odd_out[0] = join(times_rows(tall, own_w[BENEATH_R]))
            send_rows(odd_out.at[0], s, state_role, 0, 1, odd_send.at[0], skip_own=True)

            @pl.when(state_role)
            def _():
                state_in[0, 1, c] = odd_out[0, states_of(c)]

            @pl.when(row_role)
            def _():
                row_in[0, 1, c] = odd_out[0]

        def odd_above():
            @pl.when(has_next)
            def _():
                odd_out[1] = join(times_rows(tall, own_w[ABOVE_R]))
                send_rows(
                    odd_out.at[1], s + 2, level_next > ROW_LEVELS, 0, 0, odd_send.at[1]
                )

        @pl.when(chip % 2 == 1)
        def _():
            odd_beneath()
            odd_above()

        @pl.when(chip % 2 == 0)
        def _():
            odd_above()
            odd_beneath()

        def let_go():
            pl.semaphore_signal(go, inc=1, device_id=(s - 1, c), device_id_type=MESH)

        @pl.when(state_role)
        def _():
            let_go()

        pivot_odd[...] = join(times_rows(tall, own_w[PIVOT]))

        odd_pair = (e // reach // 2) % 2

        def convert(index):
            arrived(state_raw.at[index], mat_recv.at[index])
            for part in range(2):
                for k in range(parts):
                    at = (part * parts + k) * rows
                    high, low = split(state_raw[index, k, part])
                    state_w[index, :, at : at + rows] = high
                    state_w[index, :, 2 * depth + at : 2 * depth + at + rows] = low

        def state_product(index, pieces):
            return join(times_columns(split_tall(side_by_side(pieces)), state_w[index]))

        @pl.when(state_role)
        def _():
            @pl.when(not_root)
            def _():
                @pl.loop(0, 2)
                def _(index):
                    convert(index)

            arrived(rhs_state, rhs_recv)
            arrived(state_in.at[0, 1, pl.ds(0, parts - 1)], reduce_recv.at[0, 1])
            state_x[...] = rhs_state[...] - state_in[0, 1]

            @pl.when(not_root)
            def _():
                arrived(state_in.at[0, 0], reduce_recv.at[0, 0])
                state_x[...] -= state_in[0, 0]

            @pl.loop(1, level)
            def _(j):
                arrived(state_in.at[j, 1], reduce_recv.at[j, 1])
                state_x[...] -= state_in[j, 1]

                @pl.when(not_root)
                def _():
                    arrived(state_in.at[j, 0], reduce_recv.at[j, 0])
                    state_x[...] -= state_in[j, 0]

            @pl.when(not_root)
            def _():
                @pl.loop(0, 2)
                def _(turn_id):
                    side = jnp.where(odd_pair == 1, turn_id, 1 - turn_id)
                    target = e + (2 * side - 1) * reach

                    @pl.when(target < slabs)
                    def _():
                        product = state_product(side, state_x[...])
                        for k in range(parts):
                            state_out[side, k] = product[:, k * rows : (k + 1) * rows]
                        send(
                            state_out.at[side],
                            state_in.at[level, 1 - side],
                            up_send.at[side],
                            reduce_recv.at[level, 1 - side],
                            (target + 1, c),
                        )

        @pl.when(row_role)
        def _():
            for index in (BENEATH_R, ABOVE_R):
                arrived(row_raw.at[index], mat_recv.at[index])
                row_w[index] = stacked(row_raw[index])
            arrived(rhs_row, rhs_recv)
            arrived(row_in.at[0, 1, pl.ds(0, parts - 1)], reduce_recv.at[0, 1])
            arrived(row_in.at[0, 0], reduce_recv.at[0, 0])
            row_x[...] = rhs_row[...] - row_in[0, 1] - row_in[0, 0]

            for j in range(1, ROW_LEVELS):
                @pl.when(level > j)
                def _():
                    arrived(row_in.at[j, 1], reduce_recv.at[j, 1])
                    arrived(row_in.at[j, 0], reduce_recv.at[j, 0])
                    row_x[...] -= row_in[j, 1] + row_in[j, 0]

            row_tall = split_tall(side_by_side(row_x[...]))

            @pl.loop(0, 2)
            def _(turn_id):
                side = jnp.where(odd_pair == 1, turn_id, 1 - turn_id)
                target = e + (2 * side - 1) * reach

                @pl.when(target < slabs)
                def _():
                    row_out[side] = join(times_rows(row_tall, row_w[side]))
                    target_level, _ = place_of(target, levels)
                    send_rows(
                        row_out.at[side],
                        target + 1,
                        target_level > ROW_LEVELS,
                        level,
                        1 - side,
                        up_send.at[side],
                    )

            let_go()
            state_x[...] = row_x[:, states_of(c)]

        convert(PIVOT)
        product = state_product(PIVOT, state_x[...])
        for k in range(parts):
            solved[k] = product[:, k * rows : (k + 1) * rows]

        @pl.when(not_root)
        def _():
            @pl.loop(BENEATH_S, ABOVE_S + 1)
            def _(index):
                convert(index)

            @pl.loop(0, 2)
            def _(turn_id):
                side = jnp.where(odd_pair == 1, 1 - turn_id, turn_id)

                @pl.when(e + (2 * side - 1) * reach < slabs)
                def _():
                    arrived(solve_in.at[side], solve_recv.at[side])
                    product = state_product(BENEATH_S + side, solve_in[side])
                    for k in range(parts):
                        solved[k] -= product[:, k * rows : (k + 1) * rows]

        def send_solved(j, side):
            target = s + (2 * side - 1) * jnp.left_shift(jnp.int32(1), j)
            send(
                solved, solve_in.at[1 - side], solve_send.at[j, side],
                solve_recv.at[1 - side], (target, c),
            )

        @pl.loop(0, level - 1)
        def _(i):
            j = level - 1 - i
            send_solved(j, 1)

            @pl.when(not_root)
            def _():
                send_solved(j, 0)

        @pl.when(not_root)
        def _():
            around(
                s - 2,
                lambda device: send(
                    solved, odd_in.at[1, :, states_of(c)], last_send.at[1], last_recv.at[1], device
                ),
            )

        around(
            s,
            lambda device: send(
                solved, odd_in.at[0, :, states_of(c)], last_send.at[0], last_recv.at[0], device
            ),
            skip_own=True,
        )
        odd_in[0, :, states_of(c)] = solved[...]
        around(
            s - 1,
            lambda device: send(
                solved.at[device[1]], out_in.at[states_of(c)], out_send, out_recv, device
            ),
        )

        def settle(side):
            def take():
                if side == 0:
                    arrived(solved_three, last_recv.at[0])
                else:
                    arrived(odd_in.at[1], last_recv.at[1])
                pivot_odd[...] -= join(
                    times_rows(split_tall(side_by_side(odd_in[side])), own_w[BENEATH_S + side])
                )

            if side == 0:
                take()
            else:
                pl.when(has_next)(take)

        solved_three = psi_full.at[pl.ds(0, parts - 1)]

        @pl.when(chip % 2 == 1)
        def _():
            settle(1)
            settle(0)

        @pl.when(chip % 2 == 0)
        def _():
            settle(0)
            settle(1)

        out[0] = pivot_odd[...].T

        arrived(psi_full.at[pl.ds(0, parts - 1)], psi_send)
        arrived(x_full.at[pl.ds(0, parts - 1)], x_send)
        arrived(next_full, next_send)

        @pl.when(state_role)
        def _():
            arrived(rhs_state.at[pl.ds(0, parts - 1)], odd_send.at[0])

        @pl.when(row_role)
        def _():
            arrived(rhs_row.at[pl.ds(0, parts - 1)], odd_send.at[0])

        @pl.when(has_next)
        def _():
            arrived(prev_parts, prev_send)

            @pl.when(level_next > ROW_LEVELS)
            def _():
                arrived(rhs_state, odd_send.at[1])

            @pl.when(level_next <= ROW_LEVELS)
            def _():
                arrived(rhs_row, odd_send.at[1])

        @pl.when(not_root)
        def _():
            @pl.loop(0, 2)
            def _(side):
                target = e + (2 * side - 1) * reach
                target_level, _ = place_of(target, levels)

                @pl.when(target < slabs)
                def _():
                    small = target_level > ROW_LEVELS

                    @pl.when(small)
                    def _():
                        arrived(rhs_state, up_send.at[side])

                    @pl.when(jnp.logical_not(small))
                    def _():
                        arrived(rhs_row, up_send.at[side])

            arrived(rhs_row, last_send.at[1])

        arrived(psi_full.at[pl.ds(0, parts - 1)], last_send.at[0])
        arrived(rhs_state, out_send)

        @pl.loop(1, level)
        def _(j):
            arrived(solved, solve_send.at[j, 1])

            @pl.when(not_root)
            def _():
                arrived(solved, solve_send.at[j, 0])


def per_device(*args):
    slabs = lax.axis_size("slab")
    levels = slabs.bit_length() - 1
    parts = lax.axis_size("col")
    psi = args[0]
    rows, width = psi.shape[1:]
    depth = parts * rows
    quarter = width // parts
    f32, bf16 = jnp.float32, jnp.bfloat16

    def whole(*lead):
        return pltpu.VMEM((*lead, parts, width, rows), f32)

    def piece(*lead):
        return pltpu.VMEM((*lead, parts, quarter, rows), f32)

    dma = pltpu.SemaphoreType.DMA
    return pl.pallas_call(
        functools.partial(kernel, slabs, levels, parts),
        out_shape=jax.ShapeDtypeStruct(psi.shape, psi.dtype),
        in_specs=[pl.BlockSpec(memory_space=pl.ANY)] * len(args),
        out_specs=pl.BlockSpec(memory_space=pltpu.VMEM),
        scratch_shapes=[
            pltpu.VMEM((rows, width), f32),
            pltpu.VMEM((rows, depth), f32),
            pltpu.VMEM((rows, depth), f32),
            pltpu.VMEM((5, 2, rows, depth), f32),
            pltpu.VMEM((5, 2, depth, rows), f32),
            whole(),
            whole(),
            whole(),
            whole(),
            whole(),
            pltpu.VMEM((2 * rows, depth), bf16),
            pltpu.VMEM((2 * rows, depth), bf16),
            pltpu.VMEM((5, 4 * rows, depth), bf16),
            pltpu.VMEM((2, 2, rows, depth), f32),
            pltpu.VMEM((2, 4 * rows, depth), bf16),
            pltpu.VMEM((5, parts, 2, depth, rows), f32),
            pltpu.VMEM((5, depth, 4 * depth), bf16),
            pltpu.VMEM((width, rows), f32),
            pltpu.VMEM((2, width, rows), f32),
            whole(),
            whole(ROW_LEVELS, 2),
            whole(),
            pltpu.VMEM((2, width, rows), f32),
            piece(),
            piece(levels, 2),
            piece(),
            piece(2),
            piece(2),
            piece(),
            whole(2),
            pltpu.VMEM((width, rows), f32),
            dma((8,)),
            *[dma] * 10,
            dma((5,)),
            dma((5,)),
            dma((2,)),
            dma((2,)),
            dma((levels, 2)),
            dma((levels, 2)),
            dma((2,)),
            dma((2,)),
            dma((2,)),
            dma,
            dma,
            pltpu.SemaphoreType.REGULAR,
        ],
        compiler_params=pltpu.CompilerParams(
            collective_id=0, has_side_effects=True, vmem_limit_bytes=56 * 2**20
        ),
    )(*args)


def solution(mesh):
    vector = P("slab", "col", None)
    block = P("slab", None, "col", None)
    return jax.shard_map(
        per_device,
        mesh=mesh,
        in_specs=(vector,) * 3 + (block,) * 5,
        out_specs=vector,
        check_vma=False,
    )
```

time: 501 us -> 111 us (0.22)
  the two profiles are of different devices: /device:TPU:32 before, /device:TPU:1 now
where the time goes in v4:
time: 111 us
  Pallas kernels  110 us (99%)
  local copies, waits for them, and re-layouts  1.47 us (1%)
    pallas_call x1, Pallas kernels, per_device(): pl.pallas_call(functools.partial(kernel, slabs, levels, parts), out_shape...  110 us

profile of v4, /device:TPU:1, one launch (start us, length us, event | category | flops | bytes accessed | tf_op | source)
XLA Modules:
  0.0 111.2 jit_solution(5277762005056622209)
XLA Ops:
  0.0 109.7 %shard_map.82 = f32[1,128,128]{2,1,0:T(8,128)} custom-call(f32[1,128,128]{2,1,0:T(8,128)} %refs_0_.1, f32[1,128,512]{2,1,0:T(8,128)} %refs_1_.1, f32[1,128,512]{2,1,0:T(8,128)} %refs_2_.1, f32[1,2,128,512]{3,2,1,0:T(8,128)} %refs_3_.1, f32[1,2,128,512]{3,2,1,0:T(8,128)} %refs_4_.1, f32[1,2,128,512]{3,2,1,0:T(8,128)} %refs_5_.1, f32[1,2,128,512]{3,2,1,0:T(8,128)} %refs_6_.1, ...), custom_call_target="tpu_custom_call" | custom-call | tf_op jit(solution)/shard_map/pallas_call | solution.py:690
  109.7 1.5 %copy.10 = f32[1,128,128]{2,1,0:T(8,128)} copy(f32[1,128,128]{2,1,0:T(8,128)} %shard_map.82) | data formatting | bytes 131072

commit v5 on v4

--- a/solution.py
+++ b/solution.py
@@ -76,10 +76,11 @@
         pivot_odd, odd_out,
         rhs_row, row_in, row_x, row_out,
         rhs_state, state_in, state_x, state_out,
-        solve_in, solved, odd_in, out_in,
+        solve_in, solved, odd_in, out_in, pivot_rows,
         load_sem, psi_send, psi_recv, next_send, next_recv, prev_send, prev_recv,
         x_send, x_recv, rhs_send, rhs_recv, mat_send, mat_recv, odd_send, up_send,
-        reduce_recv, solve_send, solve_recv, last_send, last_recv, out_send, out_recv, go,
+        reduce_recv, solve_send, solve_recv, last_send, last_recv, out_send, out_recv,
+        gather_send, gather_recv, part_send, part_recv, go,
     ) = refs
     s = lax.axis_index("slab")
     c = lax.axis_index("col")
@@ -91,6 +92,7 @@
     level_next, _ = place_of(e + 2, levels)
     is_root = e == 0
     not_root = e > 0
+    has_above = e + reach < slabs
     state_role = level > ROW_LEVELS
     row_role = level <= ROW_LEVELS
     has_next = e + 2 < slabs
@@ -235,21 +237,37 @@
             ),
         )
 
+    def hand_over(index):
+        send(
+            blocks_v.at[index], row_raw.at[index], mat_send.at[index], mat_recv.at[index],
+            (s + 1, c),
+        )
+
     @pl.when(even)
     def _():
-        @pl.when(row_role)
-        def _():
-            for index in (BENEATH_R, ABOVE_R):
-                send(
-                    blocks_v.at[index], row_raw.at[index], mat_send.at[index],
-                    mat_recv.at[index], (s + 1, c),
-                )
-
-        @pl.when(jnp.logical_and(state_role, not_root))
-        def _():
-            for index in (BENEATH_R, ABOVE_R):
-                turn(index)
-                pass_on(index)
+        @pl.when(is_root)
+        def _():
+            turn(PIVOT)
+            pass_on(PIVOT)
+
+        @pl.when(not_root)
+        def _():
+            hand_over(PIVOT)
+
+            @pl.when(row_role)
+            def _():
+                hand_over(BENEATH_R)
+                hand_over(ABOVE_R)
+
+            @pl.when(state_role)
+            def _():
+                turn(BENEATH_R)
+                pass_on(BENEATH_R)
+
+                @pl.when(has_above)
+                def _():
+                    turn(ABOVE_R)
+                    pass_on(ABOVE_R)
 
     @pl.when(odd)
     def _():
@@ -289,20 +307,20 @@
                 lambda device: send(x_full.at[c], rhs_row.at[c], rhs_send, rhs_recv, device),
             )
 
-        turn(PIVOT)
-
         @pl.when(not_root)
         def _():
             turn(BENEATH_S)
             turn(ABOVE_S)
 
         pl.semaphore_wait(go, 1)
-        pass_on(PIVOT)
 
         @pl.when(not_root)
         def _():
             pass_on(BENEATH_S)
-            pass_on(ABOVE_S)
+
+            @pl.when(has_above)
+            def _():
+                pass_on(ABOVE_S)
 
         arrived(out_in, out_recv)
         out[0] = out_in[...].T
@@ -314,14 +332,28 @@
         def _():
             arrived(next_full, next_send)
             arrived(state_raw.at[BENEATH_S], mat_send.at[BENEATH_S])
-            arrived(state_raw.at[ABOVE_S], mat_send.at[ABOVE_S])
+            arrived(row_raw.at[PIVOT], mat_send.at[PIVOT])
+
+            @pl.when(has_above)
+            def _():
+                arrived(state_raw.at[ABOVE_S], mat_send.at[ABOVE_S])
 
             @pl.when(state_role)
             def _():
                 arrived(state_raw.at[BENEATH_R], mat_send.at[BENEATH_R])
-                arrived(state_raw.at[ABOVE_R], mat_send.at[ABOVE_R])
-
-        arrived(state_raw.at[PIVOT], mat_send.at[PIVOT])
+
+                @pl.when(has_above)
+                def _():
+                    arrived(state_raw.at[ABOVE_R], mat_send.at[ABOVE_R])
+
+            @pl.when(row_role)
+            def _():
+                arrived(row_raw.at[BENEATH_R], mat_send.at[BENEATH_R])
+                arrived(row_raw.at[ABOVE_R], mat_send.at[ABOVE_R])
+
+        @pl.when(is_root)
+        def _():
+            arrived(state_raw.at[PIVOT], mat_send.at[PIVOT])
 
         @pl.when(state_role)
         def _():
@@ -330,8 +362,6 @@
         @pl.when(row_role)
         def _():
             arrived(rhs_row, rhs_send)
-            arrived(row_raw.at[BENEATH_R], mat_send.at[BENEATH_R])
-            arrived(row_raw.at[ABOVE_R], mat_send.at[ABOVE_R])
 
     @pl.when(odd)
     def _():
@@ -432,6 +462,11 @@
                     state_w[index, :, at : at + rows] = high
                     state_w[index, :, 2 * depth + at : 2 * depth + at + rows] = low
 
+        def convert_pair(first):
+            @pl.loop(first, first + 1 + has_above.astype(jnp.int32))
+            def _(index):
+                convert(index)
+
         def state_product(index, pieces):
             return join(times_columns(split_tall(side_by_side(pieces)), state_w[index]))
 
@@ -439,9 +474,7 @@
         def _():
             @pl.when(not_root)
             def _():
-                @pl.loop(0, 2)
-                def _(index):
-                    convert(index)
+                convert_pair(BENEATH_R)
 
             arrived(rhs_state, rhs_recv)
             arrived(state_in.at[0, 1, pl.ds(0, parts - 1)], reduce_recv.at[0, 1])
@@ -520,18 +553,43 @@
                     )
 
             let_go()
-            state_x[...] = row_x[:, states_of(c)]
-
-        convert(PIVOT)
-        product = state_product(PIVOT, state_x[...])
-        for k in range(parts):
-            solved[k] = product[:, k * rows : (k + 1) * rows]
+
+        @pl.when(is_root)
+        def _():
+            convert(PIVOT)
+            product = state_product(PIVOT, state_x[...])
+            for k in range(parts):
+                solved[k] = product[:, k * rows : (k + 1) * rows]
 
         @pl.when(not_root)
         def _():
-            @pl.loop(BENEATH_S, ABOVE_S + 1)
-            def _(index):
-                convert(index)
+            @pl.when(state_role)
+            def _():
+                around(
+                    s,
+                    lambda device: send(
+                        state_x, row_x.at[:, states_of(c)], gather_send, gather_recv, device
+                    ),
+                    skip_own=True,
+                )
+                row_x[:, states_of(c)] = state_x[...]
+                arrived(psi_full.at[pl.ds(0, parts - 1)], gather_recv)
+
+            arrived(row_raw.at[PIVOT], mat_recv.at[PIVOT])
+            row_w[PIVOT] = stacked(row_raw[PIVOT])
+            pivot_rows[...] = join(
+                times_rows(split_tall(side_by_side(row_x[...])), row_w[PIVOT])
+            )
+            around(
+                s,
+                lambda device: send(
+                    pivot_rows.at[states_of(device[1])], solved.at[c], part_send, part_recv, device
+                ),
+                skip_own=True,
+            )
+            solved[c] = pivot_rows[states_of(c)]
+            convert_pair(BENEATH_S)
+            arrived(rhs_state.at[pl.ds(0, parts - 1)], part_recv)
 
             @pl.loop(0, 2)
             def _(turn_id):
@@ -660,6 +718,14 @@
 
         arrived(psi_full.at[pl.ds(0, parts - 1)], last_send.at[0])
         arrived(rhs_state, out_send)
+
+        @pl.when(not_root)
+        def _():
+            arrived(rhs_state.at[pl.ds(0, parts - 1)], part_send)
+
+            @pl.when(state_role)
+            def _():
+                arrived(psi_full.at[pl.ds(0, parts - 1)], gather_send)
 
         @pl.loop(1, level)
         def _(j):
@@ -706,8 +772,8 @@
             pltpu.VMEM((2 * rows, depth), bf16),
             pltpu.VMEM((2 * rows, depth), bf16),
             pltpu.VMEM((5, 4 * rows, depth), bf16),
-            pltpu.VMEM((2, 2, rows, depth), f32),
-            pltpu.VMEM((2, 4 * rows, depth), bf16),
+            pltpu.VMEM((3, 2, rows, depth), f32),
+            pltpu.VMEM((3, 4 * rows, depth), bf16),
             pltpu.VMEM((5, parts, 2, depth, rows), f32),
             pltpu.VMEM((5, depth, 4 * depth), bf16),
             pltpu.VMEM((width, rows), f32),
@@ -724,6 +790,7 @@
             piece(),
             whole(2),
             pltpu.VMEM((width, rows), f32),
+            pltpu.VMEM((width, rows), f32),
             dma((8,)),
             *[dma] * 10,
             dma((5,)),
@@ -737,6 +804,7 @@
             dma((2,)),
             dma,
             dma,
+            *[dma] * 4,
             pltpu.SemaphoreType.REGULAR,
         ],
         compiler_params=pltpu.CompilerParams(

time: 111 us -> 99.1 us (0.89)
  Pallas kernels: 110 us -> 97.4 us
    pallas_call x1, Pallas kernels: 110 us -> 97.4 us  [per_device(): pl.pallas_call(functools.partial(kernel, slabs, levels, parts), out_shape...]
where the time goes in v5:
time: 99.1 us; the launch traced here: 98.9 us
  Pallas kernels  97.4 us (98%)
  local copies, waits for them, and re-layouts  1.47 us (1%)
    pallas_call x1, Pallas kernels, per_device(): pl.pallas_call(functools.partial(kernel, slabs, levels, parts), out_shape...  97.4 us

profile of v5, /device:TPU:1, one launch (start us, length us, event | category | flops | bytes accessed | tf_op | source)
XLA Modules:
  0.0 98.9 jit_solution(6594796998025502763)
XLA Ops:
  0.0 97.4 %shard_map.82 = f32[1,128,128]{2,1,0:T(8,128)} custom-call(f32[1,128,128]{2,1,0:T(8,128)} %refs_0_.1, f32[1,128,512]{2,1,0:T(8,128)} %refs_1_.1, f32[1,128,512]{2,1,0:T(8,128)} %refs_2_.1, f32[1,2,128,512]{3,2,1,0:T(8,128)} %refs_3_.1, f32[1,2,128,512]{3,2,1,0:T(8,128)} %refs_4_.1, f32[1,2,128,512]{3,2,1,0:T(8,128)} %refs_5_.1, f32[1,2,128,512]{3,2,1,0:T(8,128)} %refs_6_.1, ...), custom_call_target="tpu_custom_call" | custom-call | tf_op jit(solution)/shard_map/pallas_call | solution.py:756
  97.4 1.5 %copy.10 = f32[1,128,128]{2,1,0:T(8,128)} copy(f32[1,128,128]{2,1,0:T(8,128)} %shard_map.82) | data formatting | bytes 131072

commit v6 on v5

--- a/solution.py
+++ b/solution.py
@@ -9,7 +9,7 @@
 
 MESH = pl.DeviceIdType.MESH
 half_step = 0.5
-ROW_LEVELS = 2
+ROW_LEVELS = 3
 BENEATH_R, ABOVE_R, PIVOT, BENEATH_S, ABOVE_S = range(5)
 
 
@@ -137,19 +137,19 @@
     def greet(device):
         pl.semaphore_signal(barrier, inc=1, device_id=device, device_id_type=MESH)
 
+    expected = jnp.int32(2 * parts - 1)
+
+    @pl.when(jnp.logical_and(even, not_root))
+    def _():
+        around(s - 1, greet)
+
+    @pl.when(jnp.logical_and(odd, has_next))
+    def _():
+        around(s + 1, greet)
+
+    expected += parts * jnp.where(odd, has_next, not_root).astype(jnp.int32)
+    around(s + 1 - 2 * (s % 2), greet)
     around(s, greet, skip_own=True)
-    around(s + 1 - 2 * (s % 2), greet)
-    expected = jnp.int32(2 * parts - 1)
-
-    @pl.when(jnp.logical_and(even, not_root))
-    def _():
-        around(s - 1, greet)
-
-    @pl.when(jnp.logical_and(odd, has_next))
-    def _():
-        around(s + 1, greet)
-
-    expected += parts * jnp.where(odd, has_next, not_root).astype(jnp.int32)
     for j in range(1, levels):
         for sign in (-1, 1):
             target = s + sign * 2**j
@@ -453,22 +453,30 @@
 
         odd_pair = (e // reach // 2) % 2
 
+        pieces = parts // 2
+
         def convert(index):
             arrived(state_raw.at[index], mat_recv.at[index])
             for part in range(2):
                 for k in range(parts):
-                    at = (part * parts + k) * rows
+                    half, place = k // pieces, k % pieces
+                    at = (part * pieces + place) * rows
                     high, low = split(state_raw[index, k, part])
-                    state_w[index, :, at : at + rows] = high
-                    state_w[index, :, 2 * depth + at : 2 * depth + at + rows] = low
+                    state_w[index, half, :, at : at + rows] = high
+                    state_w[index, half, :, depth + at : depth + at + rows] = low
 
         def convert_pair(first):
             @pl.loop(first, first + 1 + has_above.astype(jnp.int32))
             def _(index):
                 convert(index)
 
-        def state_product(index, pieces):
-            return join(times_columns(split_tall(side_by_side(pieces)), state_w[index]))
+        def by_halves(index, vectors, take):
+            tall = split_tall(side_by_side(vectors))
+            for half in range(2):
+                product = join(times_columns(tall, state_w[index, half]))
+                for place in range(pieces):
+                    take(half * pieces + place, product[:, place * rows : (place + 1) * rows])
+                yield pl.ds(half * pieces, pieces)
 
         @pl.when(state_role)
         def _():
@@ -504,16 +512,17 @@
 
                     @pl.when(target < slabs)
                     def _():
-                        product = state_product(side, state_x[...])
-                        for k in range(parts):
-                            state_out[side, k] = product[:, k * rows : (k + 1) * rows]
-                        send(
-                            state_out.at[side],
-                            state_in.at[level, 1 - side],
-                            up_send.at[side],
-                            reduce_recv.at[level, 1 - side],
-                            (target + 1, c),
-                        )
+                        def put(k, product):
+                            state_out[side, k] = product
+
+                        for half in by_halves(side, state_x[...], put):
+                            send(
+                                state_out.at[side, half],
+                                state_in.at[level, 1 - side, half],
+                                up_send.at[side],
+                                reduce_recv.at[level, 1 - side],
+                                (target + 1, c),
+                            )
 
         @pl.when(row_role)
         def _():
@@ -554,12 +563,36 @@
 
             let_go()
 
+        def send_solved(j, side, half):
+            target = s + (2 * side - 1) * jnp.left_shift(jnp.int32(1), j)
+            send(
+                solved.at[half], solve_in.at[1 - side, half], solve_send.at[j, side],
+                solve_recv.at[1 - side], (target, c),
+            )
+
+        def send_tier(j, half):
+            send_solved(j, 1, half)
+
+            @pl.when(not_root)
+            def _():
+                send_solved(j, 0, half)
+
+        def first_tier(half):
+            @pl.when(level > 1)
+            def _():
+                send_tier(level - 1, half)
+
+        def put_solved(k, product):
+            solved[k] = product
+
+        def take_off(k, product):
+            solved[k] -= product
+
         @pl.when(is_root)
         def _():
             convert(PIVOT)
-            product = state_product(PIVOT, state_x[...])
-            for k in range(parts):
-                solved[k] = product[:, k * rows : (k + 1) * rows]
+            for half in by_halves(PIVOT, state_x[...], put_solved):
+                first_tier(half)
 
         @pl.when(not_root)
         def _():
@@ -591,32 +624,22 @@
             convert_pair(BENEATH_S)
             arrived(rhs_state.at[pl.ds(0, parts - 1)], part_recv)
 
-            @pl.loop(0, 2)
-            def _(turn_id):
-                side = jnp.where(odd_pair == 1, 1 - turn_id, turn_id)
-
-                @pl.when(e + (2 * side - 1) * reach < slabs)
-                def _():
-                    arrived(solve_in.at[side], solve_recv.at[side])
-                    product = state_product(BENEATH_S + side, solve_in[side])
-                    for k in range(parts):
-                        solved[k] -= product[:, k * rows : (k + 1) * rows]
-
-        def send_solved(j, side):
-            target = s + (2 * side - 1) * jnp.left_shift(jnp.int32(1), j)
-            send(
-                solved, solve_in.at[1 - side], solve_send.at[j, side],
-                solve_recv.at[1 - side], (target, c),
-            )
-
-        @pl.loop(0, level - 1)
+            early = jnp.where(jnp.logical_or(odd_pair == 1, jnp.logical_not(has_above)), 1, 0)
+            last = 1 - early
+
+            @pl.when(jnp.logical_or(early == 0, has_above))
+            def _():
+                arrived(solve_in.at[early], solve_recv.at[early])
+                for _ in by_halves(BENEATH_S + early, solve_in[early], take_off):
+                    pass
+
+            arrived(solve_in.at[last], solve_recv.at[last])
+            for half in by_halves(BENEATH_S + last, solve_in[last], take_off):
+                first_tier(half)
+
+        @pl.loop(1, level - 1)
         def _(i):
-            j = level - 1 - i
-            send_solved(j, 1)
-
-            @pl.when(not_root)
-            def _():
-                send_solved(j, 0)
+            send_tier(level - 1 - i, pl.ds(0, parts))
 
         @pl.when(not_root)
         def _():
@@ -775,7 +798,7 @@
             pltpu.VMEM((3, 2, rows, depth), f32),
             pltpu.VMEM((3, 4 * rows, depth), bf16),
             pltpu.VMEM((5, parts, 2, depth, rows), f32),
-            pltpu.VMEM((5, depth, 4 * depth), bf16),
+            pltpu.VMEM((5, 2, depth, 2 * depth), bf16),
             pltpu.VMEM((width, rows), f32),
             pltpu.VMEM((2, width, rows), f32),
             whole(),

time: 99.1 us -> 97 us (0.979)
  Pallas kernels: 97.4 us -> 95.4 us
    pallas_call x1, Pallas kernels: 97.4 us -> 95.4 us  [per_device(): pl.pallas_call(functools.partial(kernel, slabs, levels, parts), out_shape...]
where the time goes in v6:
time: 97 us; the launch traced here: 96.9 us
  Pallas kernels  95.4 us (98%)
  local copies, waits for them, and re-layouts  1.47 us (2%)
    pallas_call x1, Pallas kernels, per_device(): pl.pallas_call(functools.partial(kernel, slabs, levels, parts), out_shape...  95.4 us

profile of v6, /device:TPU:1, one launch (start us, length us, event | category | flops | bytes accessed | tf_op | source)
XLA Modules:
  0.0 96.9 jit_solution(12130625717060683797)
XLA Ops:
  0.0 95.4 %shard_map.82 = f32[1,128,128]{2,1,0:T(8,128)} custom-call(f32[1,128,128]{2,1,0:T(8,128)} %refs_0_.1, f32[1,128,512]{2,1,0:T(8,128)} %refs_1_.1, f32[1,128,512]{2,1,0:T(8,128)} %refs_2_.1, f32[1,2,128,512]{3,2,1,0:T(8,128)} %refs_3_.1, f32[1,2,128,512]{3,2,1,0:T(8,128)} %refs_4_.1, f32[1,2,128,512]{3,2,1,0:T(8,128)} %refs_5_.1, f32[1,2,128,512]{3,2,1,0:T(8,128)} %refs_6_.1, ...), custom_call_target="tpu_custom_call" | custom-call | tf_op jit(solution)/shard_map/pallas_call | solution.py:779
  95.4 1.5 %copy.10 = f32[1,128,128]{2,1,0:T(8,128)} copy(f32[1,128,128]{2,1,0:T(8,128)} %shard_map.82) | data formatting | bytes 131072

commit v7 on v6

--- a/solution.py
+++ b/solution.py
@@ -9,7 +9,7 @@
 
 MESH = pl.DeviceIdType.MESH
 half_step = 0.5
-ROW_LEVELS = 3
+ROW_LEVELS = 2
 BENEATH_R, ABOVE_R, PIVOT, BENEATH_S, ABOVE_S = range(5)
 
 
@@ -71,7 +71,7 @@
         psi_h, energy_h, tunnel_h, pivot_h, beneath_reduce_h, above_reduce_h,
         beneath_solve_h, above_solve_h, out,
         psi_raw, energy_v, tunnel_v, blocks_v, turned_v,
-        psi_full, next_full, prev_parts, prev_send_v, x_full,
+        psi_full, tunnel_in, up_rows, up_in, prev_parts, prev_send_v, x_full,
         energy_w, tunnel_w, own_w, row_raw, row_w, state_raw, state_w,
         pivot_odd, odd_out,
         rhs_row, row_in, row_x, row_out,
@@ -80,7 +80,7 @@
         load_sem, psi_send, psi_recv, next_send, next_recv, prev_send, prev_recv,
         x_send, x_recv, rhs_send, rhs_recv, mat_send, mat_recv, odd_send, up_send,
         reduce_recv, solve_send, solve_recv, last_send, last_recv, out_send, out_recv,
-        gather_send, gather_recv, part_send, part_recv, go,
+        gather_send, gather_recv, part_send, part_recv, serve_send, serve_recv, go,
     ) = refs
     s = lax.axis_index("slab")
     c = lax.axis_index("col")
@@ -194,28 +194,26 @@
             ),
         )
 
+    def send_tunnel():
+        send(tunnel_v, tunnel_in, next_send, next_recv, (s + 1, c))
+
     @pl.when(odd)
     def _():
+        @pl.when(has_next)
+        def _():
+            send_tunnel()
+
         send_psi_row()
 
     @pl.when(even)
     def _():
-        @pl.when(not_root)
-        def _():
-            around(
-                s - 1,
-                lambda device: send(
-                    psi_full.at[c], next_full.at[c], next_send, next_recv, device
-                ),
-            )
-
+        send_psi_row()
         send_prev()
-        send_psi_row()
+        send_tunnel()
 
     def stacked(block):
         return split_tall(block.reshape(2 * rows, depth))
 
-    tunnel_w[...] = split_tall(tunnel)
     loads[2].wait()
     energy_w[...] = split_tall(energy_v[...])
     for index in range(5):
@@ -275,7 +273,19 @@
         own_w[ABOVE_R] = stacked(blocks_v[ABOVE_R])
 
     arrived(psi_full.at[pl.ds(0, parts - 1)], psi_recv)
-    x_full[c] = times_rows(split_tall(side_by_side(psi_full[...])), energy_w[...])
+    psi_tall = split_tall(side_by_side(psi_full[...]))
+
+    def serve_beneath():
+        arrived(tunnel_in, next_recv)
+        tunnel_w[...] = split_tall(tunnel_in[...])
+        up_rows[...] = times_rows(psi_tall, tunnel_w[...])
+        send(up_rows, up_in, serve_send, serve_recv, (s - 1, c))
+
+    @pl.when(jnp.logical_and(even, not_root))
+    def _():
+        serve_beneath()
+
+    x_full[c] = times_rows(psi_tall, energy_w[...])
 
     @pl.when(s > 0)
     def _():
@@ -284,8 +294,8 @@
 
     @pl.when(s + 1 < slabs)
     def _():
-        arrived(next_full, next_recv)
-        x_full[c] += times_rows(split_tall(side_by_side(next_full[...])), tunnel_w[...])
+        arrived(up_in, serve_recv)
+        x_full[c] += up_in[...]
 
     x_full[c] = psi_full[c] - half_step * rotate(x_full[c])
 
@@ -327,10 +337,11 @@
 
         arrived(psi_full.at[pl.ds(0, parts - 1)], psi_send)
         arrived(prev_parts, prev_send)
+        arrived(tunnel_in, next_send)
 
         @pl.when(not_root)
         def _():
-            arrived(next_full, next_send)
+            arrived(up_in, serve_send)
             arrived(state_raw.at[BENEATH_S], mat_send.at[BENEATH_S])
             arrived(row_raw.at[PIVOT], mat_send.at[PIVOT])
 
@@ -370,7 +381,7 @@
             lambda device: send(x_full.at[c], x_full.at[c], x_send, x_recv, device),
             skip_own=True,
         )
-        send(psi_full, next_full, next_send, next_recv, (s - 1, c))
+        serve_beneath()
 
         @pl.when(has_next)
         def _():
@@ -432,15 +443,48 @@
                     odd_out.at[1], s + 2, level_next > ROW_LEVELS, 0, 0, odd_send.at[1]
                 )
 
+        def sent_beneath():
+            @pl.when(state_role)
+            def _():
+                arrived(rhs_state.at[pl.ds(0, parts - 1)], odd_send.at[0])
+
+            @pl.when(row_role)
+            def _():
+                arrived(rhs_row.at[pl.ds(0, parts - 1)], odd_send.at[0])
+
+        def sent_above():
+            @pl.when(jnp.logical_and(has_next, level_next > ROW_LEVELS))
+            def _():
+                arrived(rhs_state, odd_send.at[1])
+
+            @pl.when(jnp.logical_and(has_next, level_next <= ROW_LEVELS))
+            def _():
+                arrived(rhs_row, odd_send.at[1])
+
         @pl.when(chip % 2 == 1)
         def _():
             odd_beneath()
+            sent_beneath()
             odd_above()
 
         @pl.when(chip % 2 == 0)
         def _():
             odd_above()
+            sent_above()
             odd_beneath()
+
+        def sent_up(side):
+            target = e + (2 * side - 1) * reach
+            target_level, _ = place_of(target, levels)
+            small = target_level > ROW_LEVELS
+
+            @pl.when(jnp.logical_and(target < slabs, small))
+            def _():
+                arrived(rhs_state, up_send.at[side])
+
+            @pl.when(jnp.logical_and(target < slabs, jnp.logical_not(small)))
+            def _():
+                arrived(rhs_row, up_send.at[side])
 
         def let_go():
             pl.semaphore_signal(go, inc=1, device_id=(s - 1, c), device_id_type=MESH)
@@ -560,6 +604,10 @@
                         1 - side,
                         up_send.at[side],
                     )
+
+                @pl.when(turn_id == 0)
+                def _():
+                    sent_up(side)
 
             let_go()
 
@@ -696,46 +744,28 @@
 
         arrived(psi_full.at[pl.ds(0, parts - 1)], psi_send)
         arrived(x_full.at[pl.ds(0, parts - 1)], x_send)
-        arrived(next_full, next_send)
-
-        @pl.when(state_role)
-        def _():
-            arrived(rhs_state.at[pl.ds(0, parts - 1)], odd_send.at[0])
-
-        @pl.when(row_role)
-        def _():
-            arrived(rhs_row.at[pl.ds(0, parts - 1)], odd_send.at[0])
+        arrived(up_in, serve_send)
+
+        @pl.when(chip % 2 == 1)
+        def _():
+            sent_above()
+
+        @pl.when(chip % 2 == 0)
+        def _():
+            sent_beneath()
 
         @pl.when(has_next)
         def _():
+            arrived(tunnel_in, next_send)
             arrived(prev_parts, prev_send)
-
-            @pl.when(level_next > ROW_LEVELS)
-            def _():
-                arrived(rhs_state, odd_send.at[1])
-
-            @pl.when(level_next <= ROW_LEVELS)
-            def _():
-                arrived(rhs_row, odd_send.at[1])
 
         @pl.when(not_root)
         def _():
             @pl.loop(0, 2)
             def _(side):
-                target = e + (2 * side - 1) * reach
-                target_level, _ = place_of(target, levels)
-
-                @pl.when(target < slabs)
+                @pl.when(jnp.logical_or(state_role, side == odd_pair))
                 def _():
-                    small = target_level > ROW_LEVELS
-
-                    @pl.when(small)
-                    def _():
-                        arrived(rhs_state, up_send.at[side])
-
-                    @pl.when(jnp.logical_not(small))
-                    def _():
-                        arrived(rhs_row, up_send.at[side])
+                    sent_up(side)
 
             arrived(rhs_row, last_send.at[1])
 
@@ -788,7 +818,9 @@
             pltpu.VMEM((5, 2, rows, depth), f32),
             pltpu.VMEM((5, 2, depth, rows), f32),
             whole(),
-            whole(),
+            pltpu.VMEM((rows, depth), f32),
+            pltpu.VMEM((width, rows), f32),
+            pltpu.VMEM((width, rows), f32),
             whole(),
             whole(),
             whole(),
@@ -827,7 +859,7 @@
             dma((2,)),
             dma,
             dma,
-            *[dma] * 4,
+            *[dma] * 6,
             pltpu.SemaphoreType.REGULAR,
         ],
         compiler_params=pltpu.CompilerParams(

time: 97 us -> 96.1 us (level)
  Pallas kernels: 95.4 us -> 94.4 us
    pallas_call x1, Pallas kernels: 95.4 us -> 94.4 us  [per_device(): pl.pallas_call(functools.partial(kernel, slabs, levels, parts), out_shape...]
where the time goes in v7:
time: 96.1 us; the launch traced here: 95.9 us
  Pallas kernels  94.4 us (98%)
  local copies, waits for them, and re-layouts  1.47 us (2%)
    pallas_call x1, Pallas kernels, per_device(): pl.pallas_call(functools.partial(kernel, slabs, levels, parts), out_shape...  94.4 us

profile of v7, /device:TPU:1, one launch (start us, length us, event | category | flops | bytes accessed | tf_op | source)
XLA Modules:
  0.0 95.9 jit_solution(12692419817662377365)
XLA Ops:
  0.0 94.4 %shard_map.82 = f32[1,128,128]{2,1,0:T(8,128)} custom-call(f32[1,128,128]{2,1,0:T(8,128)} %refs_0_.1, f32[1,128,512]{2,1,0:T(8,128)} %refs_1_.1, f32[1,128,512]{2,1,0:T(8,128)} %refs_2_.1, f32[1,2,128,512]{3,2,1,0:T(8,128)} %refs_3_.1, f32[1,2,128,512]{3,2,1,0:T(8,128)} %refs_4_.1, f32[1,2,128,512]{3,2,1,0:T(8,128)} %refs_5_.1, f32[1,2,128,512]{3,2,1,0:T(8,128)} %refs_6_.1, ...), custom_call_target="tpu_custom_call" | custom-call | tf_op jit(solution)/shard_map/pallas_call | solution.py:809
  94.4 1.5 %copy.10 = f32[1,128,128]{2,1,0:T(8,128)} copy(f32[1,128,128]{2,1,0:T(8,128)} %shard_map.82) | data formatting | bytes 131072

commit v8 on v7

--- a/solution.py
+++ b/solution.py
@@ -129,7 +129,7 @@
         load(6, beneath_solve_h.at[0], blocks_v.at[BENEATH_S]),
         load(7, above_solve_h.at[0], blocks_v.at[ABOVE_S]),
     ]
-    for copy in loads:
+    for copy in loads[:3]:
         copy.start()
 
     barrier = pltpu.get_barrier_semaphore()
@@ -167,17 +167,21 @@
                 else:
                     greet((target, c))
 
+    for copy in loads[3:]:
+        copy.start()
+
     loads[0].wait()
-    loads[1].wait()
     own = psi_raw[...].T
     psi_full[c] = own
-    tunnel = tunnel_v[...]
-    wide_tunnel = jnp.concatenate(split(tunnel), axis=1)
-    partial = times_columns(split_tall(own), wide_tunnel)
-    for k in range(parts):
-        prev_send_v[k] = partial[:, k * rows : (k + 1) * rows]
+    loads[1].wait()
 
     pl.semaphore_wait(barrier, expected)
+
+    def make_prev():
+        wide_tunnel = jnp.concatenate(split(tunnel_v[...]), axis=1)
+        partial = times_columns(split_tall(own), wide_tunnel)
+        for k in range(parts):
+            prev_send_v[k] = partial[:, k * rows : (k + 1) * rows]
 
     def send_psi_row():
         around(
@@ -204,10 +208,12 @@
             send_tunnel()
 
         send_psi_row()
+        make_prev()
 
     @pl.when(even)
     def _():
         send_psi_row()
+        make_prev()
         send_prev()
         send_tunnel()
 

time: 96.1 us -> 96 us (level)
  no operation moved by 1% of the time
where the time goes in v8:
time: 96 us; the launch traced here: 95.9 us
  Pallas kernels  94.4 us (98%)
  local copies, waits for them, and re-layouts  1.47 us (2%)
    pallas_call x1, Pallas kernels, per_device(): pl.pallas_call(functools.partial(kernel, slabs, levels, parts), out_shape...  94.4 us

profile of v8, /device:TPU:1, one launch (start us, length us, event | category | flops | bytes accessed | tf_op | source)
XLA Modules:
  0.0 95.9 jit_solution(4826263403265587245)
XLA Ops:
  0.0 94.4 %shard_map.82 = f32[1,128,128]{2,1,0:T(8,128)} custom-call(f32[1,128,128]{2,1,0:T(8,128)} %refs_0_.1, f32[1,128,512]{2,1,0:T(8,128)} %refs_1_.1, f32[1,128,512]{2,1,0:T(8,128)} %refs_2_.1, f32[1,2,128,512]{3,2,1,0:T(8,128)} %refs_3_.1, f32[1,2,128,512]{3,2,1,0:T(8,128)} %refs_4_.1, f32[1,2,128,512]{3,2,1,0:T(8,128)} %refs_5_.1, f32[1,2,128,512]{3,2,1,0:T(8,128)} %refs_6_.1, ...), custom_call_target="tpu_custom_call" | custom-call | tf_op jit(solution)/shard_map/pallas_call | solution.py:815
  94.4 1.5 %copy.10 = f32[1,128,128]{2,1,0:T(8,128)} copy(f32[1,128,128]{2,1,0:T(8,128)} %shard_map.82) | data formatting | bytes 131072

commit v9 on v8

--- a/solution.py
+++ b/solution.py
@@ -93,6 +93,7 @@
     is_root = e == 0
     not_root = e > 0
     has_above = e + reach < slabs
+    odd_pair = (e // reach // 2) % 2
     state_role = level > ROW_LEVELS
     row_role = level <= ROW_LEVELS
     has_next = e + 2 < slabs
@@ -203,11 +204,12 @@
 
     @pl.when(odd)
     def _():
+        send_psi_row()
+
         @pl.when(has_next)
         def _():
             send_tunnel()
 
-        send_psi_row()
         make_prev()
 
     @pl.when(even)
@@ -265,13 +267,14 @@
 
             @pl.when(state_role)
             def _():
-                turn(BENEATH_R)
-                pass_on(BENEATH_R)
-
-                @pl.when(has_above)
-                def _():
-                    turn(ABOVE_R)
-                    pass_on(ABOVE_R)
+                @pl.loop(0, 2)
+                def _(turn_id):
+                    side = jnp.where(odd_pair == 1, turn_id, 1 - turn_id)
+
+                    @pl.when(jnp.logical_or(side == 0, has_above))
+                    def _():
+                        turn(side)
+                        pass_on(side)
 
     @pl.when(odd)
     def _():
@@ -501,8 +504,6 @@
 
         pivot_odd[...] = join(times_rows(tall, own_w[PIVOT]))
 
-        odd_pair = (e // reach // 2) % 2
-
         pieces = parts // 2
 
         def convert(index):
@@ -532,7 +533,7 @@
         def _():
             @pl.when(not_root)
             def _():
-                convert_pair(BENEATH_R)
+                convert(jnp.where(jnp.logical_and(odd_pair == 0, has_above), ABOVE_R, BENEATH_R))
 
             arrived(rhs_state, rhs_recv)
             arrived(state_in.at[0, 1, pl.ds(0, parts - 1)], reduce_recv.at[0, 1])
@@ -562,6 +563,10 @@
 
                     @pl.when(target < slabs)
                     def _():
+                        @pl.when(jnp.logical_and(turn_id == 1, has_above))
+                        def _():
+                            convert(side)
+
                         def put(k, product):
                             state_out[side, k] = product
 

time: 96 us -> 96.1 us (level)
  no operation moved by 1% of the time
where the time goes in v9:
time: 96.1 us; the launch traced here: 95.9 us
  Pallas kernels  94.4 us (98%)
  local copies, waits for them, and re-layouts  1.47 us (2%)
    pallas_call x1, Pallas kernels, per_device(): pl.pallas_call(functools.partial(kernel, slabs, levels, parts), out_shape...  94.4 us

profile of v9, /device:TPU:1, one launch (start us, length us, event | category | flops | bytes accessed | tf_op | source)
XLA Modules:
  0.0 95.9 jit_solution(3763213918537149763)
XLA Ops:
  0.0 94.4 %shard_map.82 = f32[1,128,128]{2,1,0:T(8,128)} custom-call(f32[1,128,128]{2,1,0:T(8,128)} %refs_0_.1, f32[1,128,512]{2,1,0:T(8,128)} %refs_1_.1, f32[1,128,512]{2,1,0:T(8,128)} %refs_2_.1, f32[1,2,128,512]{3,2,1,0:T(8,128)} %refs_3_.1, f32[1,2,128,512]{3,2,1,0:T(8,128)} %refs_4_.1, f32[1,2,128,512]{3,2,1,0:T(8,128)} %refs_5_.1, f32[1,2,128,512]{3,2,1,0:T(8,128)} %refs_6_.1, ...), custom_call_target="tpu_custom_call" | custom-call | tf_op jit(solution)/shard_map/pallas_call | solution.py:820
  94.4 1.5 %copy.10 = f32[1,128,128]{2,1,0:T(8,128)} copy(f32[1,128,128]{2,1,0:T(8,128)} %shard_map.82) | data formatting | bytes 131072
